TPU v7x, 256 devices: a whole 4x4x8 slice. The times are simulated.
256 devices in a mesh: img: 64 (over x, z, core), proto: 4 (over y).
Axes of the slice: x: 4, y: 4, z: 8, core: 2. Of those that a mesh axis runs over, the one named last changes fastest.
Arguments:
- student_feats: bfloat16 [64, 128, 384], P('img'), may hold values from -1 to 1
- teacher_feats: bfloat16 [64, 128, 384], P('img'), may hold values from -1 to 1
- student_weight: bfloat16 [384, 131072], P(None, ('img', 'proto')), may hold values from -1 to 1
- teacher_weight: bfloat16 [384, 131072], P(None, ('img', 'proto')), may hold values from -1 to 1
- patch_masks: int32 [64, 128], P('img'), may hold values from 0 to 1, as said below
Outputs:
- patch_loss: float32 [], replicated
- grad_weight: float32 [384, 131072], P(None, ('img', 'proto'))
- grad_rows: float32 [4096, 384], P(('img', 'proto'))
Inputs may be any that keep to these rules, and one draw needn't show every extreme that they name: `patch_masks`: exactly 32 images have masked patches, chosen at random; a quarter of these each have 128 / 8, 32, 48 and 64 masked patches at random positions, so 1280 patches are masked in all.
All inputs are finite; a program needn't handle non-finite values.
Results may differ from a plain program's by a relative error of at most 0.0085.
Values may be sent and summed in bfloat16 or wider, within the bound.
A program may use at most 64 MiB of HBM per device.

v0:
```python
import jax
import jax.numpy as jnp
from jax import lax
from jax.sharding import PartitionSpec as P

P_SIZE = 131072
PATCH = 128
ITERS = 3


TEACHER_TEMP = 0.07
STUDENT_TEMP = 0.1
NORM_EPS = 1e-06


def slot_rows(features, mask_rows, slot_count):
    rank_of = jnp.cumsum(mask_rows, axis=1) - 1
    slot_ids = jnp.arange(slot_count, dtype=jnp.int32)
    select = (
        (mask_rows[:, None, :] == 1) & (rank_of[:, None, :] == slot_ids[None, :, None])
    ).astype(jnp.bfloat16)
    return jnp.einsum("isp,ipe->ise", select, features, preferred_element_type=jnp.float32)


def unit_rows(slot_data):
    norm_rows = jnp.sqrt(jnp.sum(slot_data * slot_data, axis=-1) + NORM_EPS)
    return ((slot_data / norm_rows[..., None]).astype(jnp.bfloat16), norm_rows)


def unit_columns(weight):
    w_float = weight.astype(jnp.float32)
    norm_cols = jnp.sqrt(jnp.sum(w_float * w_float, axis=0) + NORM_EPS)
    return ((w_float / norm_cols[None, :]).astype(jnp.bfloat16), norm_cols)


def summed_mass(row_part):
    return lax.psum(row_part, ("img", "proto"))


def shards(student_feats, teacher_feats, student_weight, teacher_weight, patch_masks):
    slot_count = PATCH // 2
    stu_local, stu_norm = unit_rows(slot_rows(student_feats, patch_masks, slot_count))
    tea_local, _ = unit_rows(slot_rows(teacher_feats, patch_masks, slot_count))
    local_counts = jnp.sum(patch_masks, axis=1).astype(jnp.bfloat16)
    stu_all, tea_all, count_all = (
        lax.all_gather(stu_local, "img", axis=0, tiled=True),
        lax.all_gather(tea_local, "img", axis=0, tiled=True),
        lax.all_gather(local_counts, "img", axis=0, tiled=True),
    )
    feature_width = stu_all.shape[-1]
    stu_flat = stu_all.reshape(-1, feature_width)
    tea_flat = tea_all.reshape(-1, feature_width)
    slot_total = stu_flat.shape[0]
    rows_total = slot_total * 5 // 16
    count_f = count_all.astype(jnp.float32)
    masked_images = jnp.sum((count_f > 0).astype(jnp.float32))
    valid_slot = (jnp.arange(slot_count, dtype=jnp.float32)[None, :] < count_f[:, None]).reshape(-1)
    slot_weight = jnp.where(
        valid_slot, 1.0 / (jnp.repeat(jnp.maximum(count_f, 1.0), slot_count) * masked_images), 0.0
    )
    w_unit, w_norm = unit_columns(student_weight)
    tea_w_unit, _ = unit_columns(teacher_weight)
    live_rows = valid_slot.astype(jnp.float32)
    logits = jnp.dot(stu_flat, w_unit, preferred_element_type=jnp.float32) / STUDENT_TEMP
    stu_exp = jnp.exp(logits)
    kernel = jnp.exp(
        jnp.dot(tea_flat, tea_w_unit, preferred_element_type=jnp.float32) / TEACHER_TEMP
    )
    row_scale = live_rows
    partition = lax.psum(jnp.sum(stu_exp, axis=1), ("img", "proto"))
    first_sweep = 0
    for sweep_idx in range(first_sweep, ITERS):
        col_scale = 1.0 / jnp.dot(row_scale, kernel, precision=lax.Precision.HIGHEST)
        row_totals = summed_mass(jnp.dot(kernel, col_scale, precision=lax.Precision.HIGHEST))
        row_scale = live_rows / jnp.where(live_rows > 0, row_totals, 1.0)
    targets = row_scale[:, None] * kernel * col_scale[None, :]
    log_part = jnp.log(partition)
    loss_part = jnp.sum(slot_weight * jnp.sum(targets * (log_part[:, None] - logits), axis=1))
    probability = stu_exp / partition[:, None]
    grad_logits = (
        slot_weight[:, None] * rows_total * (probability - targets) / STUDENT_TEMP
    ).astype(jnp.bfloat16)
    grad_unit_w = lax.dot_general(
        stu_flat, grad_logits, (((0,), (0,)), ((), ())), preferred_element_type=jnp.float32
    )
    w_float = w_unit.astype(jnp.float32)
    grad_weight = (
        P_SIZE
        / 128.0
        * (grad_unit_w - w_float * jnp.sum(w_float * grad_unit_w, axis=0)[None, :])
        / w_norm[None, :]
    )
    grad_unit_x = lax.dot_general(
        grad_logits, w_unit, (((1,), (1,)), ((), ())), preferred_element_type=jnp.float32
    )
    patch_loss = lax.psum(loss_part, ("img", "proto"))
    local_slots = stu_local.shape[0] * slot_count
    own_count = local_slots // lax.axis_size("proto")
    row_start = lax.axis_index("proto") * own_count
    own_rows = lax.psum_scatter(grad_unit_x, ("img", "proto"), scatter_dimension=0, tiled=True)
    own_unit = lax.dynamic_slice_in_dim(
        stu_local.reshape(-1, feature_width), row_start, own_count, 0
    ).astype(jnp.float32)
    own_norm = lax.dynamic_slice_in_dim(stu_norm.reshape(-1), row_start, own_count, 0)
    grad_rows = (own_rows - own_unit * jnp.sum(own_unit * own_rows, axis=1)[:, None]) / own_norm[
        :, None
    ]
    return (patch_loss, grad_weight, grad_rows)


def solution(mesh):
    placed = (
        P("img", None, None),
        P("img", None, None),
        P(None, ("img", "proto")),
        P(None, ("img", "proto")),
        P("img", None),
    )
    return jax.shard_map(
        shards,
        mesh=mesh,
        in_specs=placed,
        out_specs=(P(), P(None, ("img", "proto")), P(("img", "proto"), None)),
        check_vma=False,
    )
```

profile of v0, /device:TPU:6, one launch (start us, length us, event | category | flops | bytes accessed | tf_op | source)
XLA Modules:
  0.0 843.8 jit_solution(558506412012050554)
XLA Ops:
  7.2 0.7 compare_bitcast_fusion
  7.9 0.8 copy.9
  9.2 0.7 divide_convert_fusion.1
  10.0 1.1 multiply_reduce_fusion.1
  11.2 0.7 divide_convert_fusion
  12.0 1.3 reduce_sum.99
  13.9 1.3 dynamic-slice.7
  15.2 0.8 dynamic-update-slice
  15.9 110.6 %all-reduce = bf16[64]{0:T(256)(128)(2,1)S(1)} all-reduce(bf16[64]{0:T(256)(128)(2,1)S(1)} %dynamic-update-slice), channel_id=1, replica_groups=mesh['img'=64,'proto'=4] {'img'}, use_global_device_ids=true, to_apply=%add | all-reduce | flops 64 | bytes 256
  127.5 0.7 multiply_divide_fusion
  128.3 1.1 fusion
  129.4 1.1 fusion.2
  130.5 4.5 multiply_exponential_fusion
  135.1 3.9 fusion.29
  139.0 4.5 fusion.30
  143.5 93.2 %psum.35 = f32[4096]{0:T(1024)S(1)} all-reduce(f32[4096]{0:T(1024)S(1)} %bitcast.45), channel_id=1, replica_groups=mesh['img'=64,'proto'=4] {'img','proto'}, use_global_device_ids=true, to_apply=%region_5.6 | all-reduce | flops 4096 | bytes 32768 | tf_op jit(solution)/shard_map/psum | solution.py:37
  236.7 9.3 %fusion.31 = f32[1,512]{1,0:T(1,128)S(1)} fusion(f32[4096,1]{0,1:T(1,128)S(1)} %bitcast.43, f32[4096,512]{0,1:T(8,128)} %copy-done.1), kind=kOutput, calls=%fused_computation.62 | convolution fusion | flops 25165824 | bytes 8407040 | tf_op jit(solution)/shard_map/dot_general | solution.py:73
  246.0 4.5 fusion.32
  250.5 75.0 %psum.36 = f32[4096]{0:T(1024)S(1)} all-reduce(f32[4096]{0:T(1024)S(1)} %bitcast.46), channel_id=1, replica_groups=mesh['img'=64,'proto'=4] {'img','proto'}, use_global_device_ids=true, to_apply=%region_6.7 | all-reduce | flops 4096 | bytes 32768 | tf_op jit(solution)/shard_map/psum | solution.py:37
  325.5 9.2 %fusion.33 = f32[1,512]{1,0:T(1,128)S(1)} fusion(f32[4096,1]{0,1:T(1,128)S(1)} %bitcast.47, f32[4096,512]{0,1:T(8,128)} %copy-done.1), kind=kOutput, calls=%fused_computation.64 | convolution fusion | flops 25165824 | bytes 8407040 | tf_op jit(solution)/shard_map/dot_general | solution.py:73
  334.7 6.7 fusion.34
  341.5 7.8 exponential_reduce_fusion
  349.3 73.9 %all-reduce.1 = (f32[4096]{0:T(1024)S(1)}, f32[4096]{0:T(1024)S(1)}) all-reduce(f32[4096]{0:T(1024)S(1)} %get-tuple-element.13, f32[4096]{0:T(1024)S(1)} %bitcast.44), channel_id=1, replica_groups=mesh['img'=64,'proto'=4] {'img','proto'}, use_global_device_ids=true, to_apply=%region_11.12 | all-reduce | flops 8192 | bytes 65536 | tf_op jit(solution)/shard_map/psum | solution.py:70
  423.3 7.7 multiply_convert_fusion
  431.0 2.0 copy-done.3
  433.0 5.1 fusion.25
  438.8 74.0 %psum.39 = f32[]{:T(128)} all-reduce(f32[]{:T(128)} %multiply_reduce_fusion.3), channel_id=1, replica_groups=mesh['img'=64,'proto'=4] {'img','proto'}, use_global_device_ids=true, to_apply=%region_14.15 | all-reduce | flops 1 | bytes 8 | tf_op jit(solution)/shard_map/psum | solution.py:96
  512.9 5.0 fusion.4
  517.9 1.1 fusion.7
  519.0 315.6 %reduce-scatter.2.cloned.1.call-done = f32[16,384]{1,0:T(8,128)} async-done(((f32[4096,384]{1,0:T(8,128)}), f32[16,384]{1,0:T(8,128)}) %reduce-scatter.2.cloned.1.call-update) | async-done | bytes 24592 | tf_op jit(solution)/shard_map/reduce_scatter | solution.py:100
  834.6 0.9 fusion.17
  835.4 1.4 fusion.19
  (43 shorter events, 2.6 us)
Async XLA Ops:
  7.2 1.8 copy-start
  7.2 123.4 %all-gather.5.cloned.1.call-start = ((), (), s32[]{:S(2)}) async-start(), calls=%async_computation.2 | async-start | bytes 3194880 | tf_op jit(solution)/shard_map/all_gather | solution.py:47
  9.9 331.6 %all-gather.7.cloned.1.call-start = ((), (), s32[]{:S(2)}) async-start(), calls=%async_computation.3 | async-start | bytes 3194880 | tf_op jit(solution)/shard_map/all_gather | solution.py:46
  11.9 822.7 %reduce-scatter.2.cloned.1.call-start = ((), (), s32[]{:S(2)}) async-start(), calls=%async_computation.1 | async-start | bytes 6316032 | tf_op jit(solution)/shard_map/reduce_scatter | solution.py:100
  135.1 8.4 copy-start.1
  236.7 9.4 %copy-start.2 = (f32[4096,512]{0,1:T(8,128)S(1)}, f32[4096,512]{0,1:T(8,128)}, u32[]{:S(2)}) copy-start(f32[4096,512]{0,1:T(8,128)} %copy-done.1) | copy-start | bytes 25165828
  325.5 16.0 %copy-start.4 = (bf16[384,512]{1,0:T(8,128)(2,1)S(1)}, bf16[384,512]{1,0:T(8,128)(2,1)}, u32[]{:S(2)}) copy-start(bf16[384,512]{1,0:T(8,128)(2,1)} %param.7) | copy-start | bytes 1179652
  431.0 2.0 copy-start.3
  438.1 396.4 %copy-start.5 = (bf16[64,384]{1,0:T(8,128)(2,1)S(1)}, bf16[64,384]{1,0:T(8,128)(2,1)}, u32[]{:S(2)}) copy-start(bf16[64,384]{1,0:T(8,128)(2,1)} %divide_convert_fusion) | copy-start | bytes 147460
Sparse Core Ops, SparseCore 0:
  11.3 79.7 all-gather.4
  93.9 75.4 all-gather.6
  438.3 396.2 reduce-scatter.1
where the time goes:
time: 853 us; the launch traced here: 844 us
  blocking collectives  427 us (50%)
  waiting for transfers between devices  316 us (37%)
  matrix products  62 us (7%)
  other arithmetic  19 us (2%)
  between operations  15 us (2%)
    reduce_scatter x1, waiting for transfers between devices, shards(): lax.psum_scatter(grad_unit_x, ('img', 'proto'), scatter_dimension=0, tile...  316 us
    psum x2, blocking collectives, summed_mass(): return lax.psum(row_part, ('img', 'proto'))  168 us
    unnamed x1, blocking collectives  111 us
    psum x1, blocking collectives, shards(): patch_loss = lax.psum(loss_part, ('img', 'proto'))  74 us
    psum x1, blocking collectives, shards(): partition = lax.psum(jnp.sum(stu_exp, axis=1), ('img', 'proto'))  73.9 us
    dot_general x3, matrix products, shards(): jnp.dot(row_scale, kernel, precision=lax.Precision.HIGHEST)  22.4 us
  transfers between devices with their start and end apart: 3, of which 1 were waited for; matrix products, arithmetic and copies ran while one was open for 7% of the time, Pallas kernels for 0%

commit v1 on v0

v1 whole, which is shorter than its diff:
```python
import jax
import jax.numpy as jnp
from jax import lax
from jax.experimental import pallas as pl
from jax.experimental.pallas import tpu as pltpu
from jax.sharding import PartitionSpec as P

MESH = pl.DeviceIdType.MESH
F32, BF16 = jnp.float32, jnp.bfloat16
TEACHER_TEMP = 0.07
STUDENT_TEMP = 0.1
NORM_EPS = 1e-06
ROWS, COLS, E, ITERS = 1280, 512, 384, 3
BLK = 64
GROUPS = [(b, m) for b in range(4) for m in range(b + 1, 5)]
ROW_W = [1.0 / (16.0 * m * 32.0) for _, m in GROUPS]


def square_at(s):
    return 4 * (s % 4) + s // 4 if s < 16 else s


def split_square(o):
    kp = lax.div(o, 3)
    f = lax.rem(o, 3)
    b = lax.div(kp + 4, 8) + lax.div(kp + 1, 8) + lax.div(kp, 9)
    first = 4 * b - lax.div(b * (b - 1), 2)
    return kp, f, b, kp - first, kp - first + b + 1


def dot(a, b):
    return jnp.dot(a, b, preferred_element_type=F32)


def dot_nt(a, b):
    return lax.dot_general(a, b, (((1,), (1,)), ((), ())), preferred_element_type=F32)


def fold8(v):
    return jnp.sum(v.reshape(v.shape[0] // 8, 8, v.shape[1]), axis=0)


def kernel(
    sf, tf, sw, tw, mask,
    loss_ref, gw_ref, gr_ref,
    units, unit_f, norm_f, cnt, raw, rawc, sel, grid, tea, stu,
    w_unit, w_t, tw_t, w_norm, kt, lg, ex, gb, csum,
    a0, b0, c0, a1, b1, c1, a2, b2, c2,
    pt, core_in, summed, in_a0, in_a1, half0, half1, in_b0, in_b1, quart, in_z,
    scale, tiles, back,
    s_raw, s_cnt, r_raw, r_cnt, s_z, r_z, s_2, r_2, s_3, r_3, s_ex, r_ex,
    s_ar, r_ar, s_core, r_core, s_ra, r_ra, s_rb, r_rb, s_rz, r_rz, s_back, r_back,
):
    img = lax.axis_index("img")
    y = lax.axis_index("proto")
    c = lax.rem(img, 2)
    z = lax.rem(lax.div(img, 2), 8)
    x = lax.div(img, 16)
    is_owner = lax.rem(z, 4) == x
    h_me = lax.div(z, 4)
    o_me = 16 * h_me + 4 * x + y
    s_me = jnp.where(h_me == 0, 4 * y + x, o_me)

    def at(px, py, pz, pc):
        return ((px * 8 + pz) * 2 + pc, py)

    def x_peer(j):
        return at(lax.rem(x + j, 4), y, z, c)

    def y_peer(j):
        return at(x, lax.rem(y + j, 4), z, c)

    def z_peer(j):
        return at(x, y, lax.rem(z + j, 8), c)

    def cy_peer(j):
        g = lax.rem(c * 4 + y + j, 8)
        return at(x, lax.rem(g, 4), z, lax.div(g, 4))

    partner = at(x, y, z, 1 - c)

    def remote(src, dst, s, r, dev):
        return pltpu.make_async_remote_copy(
            src_ref=src, dst_ref=dst, send_sem=s, recv_sem=r, device_id=dev, device_id_type=MESH
        )

    bar = pltpu.get_barrier_semaphore()

    def greet(dev):
        pl.semaphore_signal(bar, inc=1, device_id=dev, device_id_type=MESH)

    for j in range(1, 4):
        greet(x_peer(j))
    for j in range(1, 8):
        greet(z_peer(j))
        greet(cy_peer(j))

    @pl.when(is_owner)
    def _():
        @pl.loop(0, 64)
        def _(i):
            @pl.when(i != img)
            def _():
                greet((i, y))

    mrow = mask[...].astype(F32)
    upper = (
        lax.broadcasted_iota(jnp.int32, (128, 128), 0) <= lax.broadcasted_iota(jnp.int32, (128, 128), 1)
    ).astype(BF16)
    mrow8 = jnp.broadcast_to(mrow, (8, 128))
    rank = dot(mrow8.astype(BF16), upper)
    cnt[...] = jnp.broadcast_to(jnp.sum(mrow, axis=1, keepdims=True), (1, 128))
    want = lax.broadcasted_iota(jnp.int32, (64, 128), 0).astype(F32)
    pick = jnp.where(
        (jnp.broadcast_to(rank[:1], (64, 128)) - 1.0 == want)
        & (jnp.broadcast_to(mrow, (64, 128)) > 0.5), 1.0, 0.0
    ).astype(BF16)

    def unit_rows(kind, feats):
        rows = dot(pick, feats[0])
        norm = jnp.sqrt(jnp.sum(rows * rows, axis=1, keepdims=True) + NORM_EPS)
        unit = (rows / norm).astype(BF16)
        for b in range(4):
            for f in range(3):
                units[kind, b, f] = unit[16 * b:16 * b + 16, 128 * f:128 * f + 128]
        return unit, norm

    s_unit, s_norm = unit_rows(0, sf)
    unit_rows(1, tf)
    for b in range(4):
        unit_f[b] = s_unit[16 * b:16 * b + 16].astype(F32)
        norm_f[b] = jnp.broadcast_to(s_norm[16 * b:16 * b + 16], (16, 128))

    @pl.when(is_owner)
    def _():
        pl.semaphore_wait(bar, 17 + 15)

    @pl.when(jnp.logical_not(is_owner))
    def _():
        pl.semaphore_wait(bar, 17 + 16)

    def each_owner(remote_fn, local_fn):
        for h in range(2):
            for px in range(4):
                for pc in range(2):
                    t = (h * 4 + px) * 2 + pc
                    to = (px * 8 + px + 4 * h) * 2 + pc
                    _, f, b, _, _ = split_square(16 * h + 4 * px + y)

                    @pl.when(img != to)
                    def _():
                        remote_fn(t, to, pc, b, f)

                    if local_fn is not None:
                        @pl.when(img == to)
                        def _():
                            local_fn(pc, b, f)

    def raw_copies(t, to, pc, b, f):
        return (
            remote(cnt, rawc.at[img], s_cnt.at[t], r_cnt, (to, y)),
            remote(units.at[pc, b, f], raw.at[img], s_raw.at[t], r_raw, (to, y)),
        )

    def raw_start(*a):
        for cp in raw_copies(*a):
            cp.start()

    def raw_done(*a):
        for cp in raw_copies(*a):
            cp.wait_send()

    def raw_local(pc, b, f):
        pltpu.make_async_copy(cnt, rawc.at[img], r_cnt).start()
        pltpu.make_async_copy(units.at[pc, b, f], raw.at[img], r_raw).start()

    each_owner(raw_start, raw_local)

    def unit_columns(w_ref):
        w = w_ref[...].astype(F32)
        norm = jnp.sqrt(jnp.sum(w * w, axis=0, keepdims=True) + NORM_EPS)
        return w / norm, norm

    tw_u, _ = unit_columns(tw)
    tw_t[...] = tw_u.T.astype(BF16)
    sw_u, sw_n = unit_columns(sw)
    w_norm[...] = sw_n
    w_unit[...] = sw_u.astype(BF16)
    w_t[...] = sw_u.T.astype(BF16)

    kp_me, f_me, b_me, k_me, m_me = split_square(o_me)

    def z_copy(j):
        return remote(grid.at[c, s_me], grid.at[c, s_me], s_z.at[j - 1], r_z.at[h_me], z_peer(j))

    @pl.when(is_owner)
    def _():
        pltpu.make_async_copy(rawc, rawc, r_cnt).wait()
        counts = rawc[:, 0, :]
        match = jnp.where(counts == (16 * m_me).astype(F32), 1.0, 0.0)
        lower = (
            lax.broadcasted_iota(jnp.int32, (64, 64), 1) < lax.broadcasted_iota(jnp.int32, (64, 64), 0)
        ).astype(BF16)
        place = jnp.where(match > 0.5, dot(lower, match.astype(BF16)), -1.0)
        lane_block = lax.shift_right_logical(lax.broadcasted_iota(jnp.int32, (64, 128), 1), 4)
        block_sel = jnp.where(place == lane_block.astype(F32), 1.0, 0.0).astype(BF16)
        spread = (
            lax.shift_right_logical(lax.broadcasted_iota(jnp.int32, (1024, 64), 0), 4)
            == lax.broadcasted_iota(jnp.int32, (1024, 64), 1)
        ).astype(BF16)
        same_row = (
            lax.bitwise_and(lax.broadcasted_iota(jnp.int32, (1024, 128), 0), 15)
            == lax.bitwise_and(lax.broadcasted_iota(jnp.int32, (1024, 128), 1), 15)
        )
        sel_f = jnp.where(same_row, dot(spread, block_sel), 0.0)
        sel[...] = sel_f
        sel_t = sel_f.T.astype(BF16)
        pltpu.make_async_copy(raw, raw, r_raw).wait()
        grid[c, s_me] = dot(sel_t, raw[...].reshape(1024, 128)).astype(BF16)
        for j in range(1, 8):
            z_copy(j).start()

    for h in range(2):
        spot = 4 * y + x if h == 0 else 16 + 4 * x + y

        @pl.when(z != x + 4 * h)
        def _():
            remote(grid.at[c, spot], grid.at[c, spot], s_z.at[0], r_z.at[h], partner).wait_recv()

    def copy2(h, j, back_j=0):
        if h == 0:
            spot = 4 * y + lax.rem(x + back_j, 4)
            dev = x_peer(j)
        else:
            spot = 16 + 4 * x + lax.rem(y + back_j, 4)
            dev = y_peer(j)
        return remote(grid.at[c, spot], grid.at[c, spot], s_2.at[h, j - 1], r_2.at[h, j - 1], dev)

    def run4(h, off):
        return pl.ds(4 * lax.rem(y + off, 4), 4) if h == 0 else pl.ds(16 + 4 * lax.rem(x + off, 4), 4)

    def copy3(h, j, back_j=0):
        run = run4(h, back_j)
        dev = y_peer(j) if h == 0 else x_peer(j)
        return remote(grid.at[c, run], grid.at[c, run], s_3.at[h, j - 1], r_3.at[h, j - 1], dev)

    def copy_ex(h, j, kind):
        run = run4(h, (4 - j) % 4)
        return remote(grid.at[kind, run], grid.at[kind, run], s_ex.at[h, j], r_ex.at[h, j], partner)

    for j in range(1, 4):
        copy2(0, j).start()
        copy2(1, j).start()
    for h in range(2):
        for j in range(1, 4):
            copy2(h, j, 4 - j).wait_recv()
        for j in range(1, 4):
            copy3(h, j).start()
    copy_ex(0, 0, c).start()
    copy_ex(1, 0, c).start()
    for j in range(1, 4):
        for h in range(2):
            copy3(h, j, 4 - j).wait_recv()
            copy_ex(h, j, c).start()
    for h in range(2):
        for j in range(4):
            copy_ex(h, j, 1 - c).wait_recv()

    for kind, feats in ((1, tea), (0, stu)):
        for s in range(30):
            o = square_at(s)
            kp, f = o // 3, o % 3
            feats[128 * kp:128 * kp + 128, 128 * f:128 * f + 128] = grid[kind, s]

    for n in range(5):
        cols = slice(256 * n, 256 * n + 256)
        k_blk = jnp.exp(dot_nt(tw_t[...], tea[cols, :]) * (1.0 / TEACHER_TEMP))
        kt[:, cols] = k_blk
        part = k_blk[:, :128] + k_blk[:, 128:]
        csum[...] = part if n == 0 else csum[...] + part
    zero8 = jnp.zeros((8, ROWS), F32)

    def first_sweep(i, acc):
        rows = pl.ds(pl.multiple_of(i * BLK, BLK), BLK)
        col = 1.0 / jnp.sum(csum[rows, :], axis=1, keepdims=True)
        return acc + fold8(kt[rows, :] * col)

    def fold1(acc):
        return jnp.sum(acc, axis=0, keepdims=True)

    tot = fold1(lax.fori_loop(0, COLS // BLK, first_sweep, zero8))

    stages = ((a0, b0, c0), (a1, b1, c1), (a2, b2, c2))
    spots = (c * 4 + y, x, z)
    sizes = (8, 4, 8)
    sem_at = (0, 7, 10)

    def ar_copy(it, st, j):
        ref = stages[it][st]
        peer = (cy_peer, x_peer, z_peer)[st](j)
        n = sem_at[st] + j - 1
        return remote(ref.at[spots[st]], ref.at[spots[st]], s_ar.at[it, n], r_ar.at[it, n], peer)

    def all_sum(it, v, fillers):
        for st in range(3):
            ref = stages[it][st]
            ref[spots[st]] = v
            for j in range(1, sizes[st]):
                ar_copy(it, st, j).start()
            fillers[st]()
            for j in range(1, sizes[st]):
                ar_copy(it, st, j).wait_recv()
            v = ref[0]
            for k in range(1, sizes[st]):
                v = v + ref[k]
        return v

    def all_sum_sent(it):
        for st in range(3):
            for j in range(1, sizes[st]):
                ar_copy(it, st, j).wait_send()

    parts = []

    def student(ns):
        for n in ns:
            cols = slice(256 * n, 256 * n + 256)
            l_blk = dot_nt(w_t[...], stu[cols, :]) * (1.0 / STUDENT_TEMP)
            lg[:, cols] = l_blk
            e_blk = jnp.exp(l_blk)
            ex[:, cols] = e_blk
            parts.append(jnp.sum(e_blk, axis=0, keepdims=True))

    def products(kind, src):
        for n in range(5):
            cols = slice(256 * n, 256 * n + 256)
            p_blk = dot(w_unit[...], src[:, cols].astype(BF16)).astype(BF16)
            for s in range(30):
                o = square_at(s)
                kp, f = o // 3, o % 3
                if kp // 2 == n:
                    lo = 128 * (kp % 2)
                    pt[kind, s] = p_blk[128 * f:128 * f + 128, lo:lo + 128]

    total = all_sum(
        0, tot, (lambda: student((0, 1)), lambda: student((2,)), lambda: student((3, 4)))
    )
    row = 1.0 / total

    def sweep(i, acc):
        rows = pl.ds(pl.multiple_of(i * BLK, BLK), BLK)
        k_blk = kt[rows, :]
        col = 1.0 / jnp.sum(k_blk * row, axis=1, keepdims=True)
        return acc + fold8(k_blk * col)

    tot = fold1(lax.fori_loop(0, COLS // BLK, sweep, zero8))
    part_mine = jnp.concatenate(parts, axis=1)

    def empty_squares():
        for kind in range(2):
            for s in (30, 31):
                pt[kind, s] = jnp.zeros((128, 128), BF16)

    total = all_sum(
        1, jnp.concatenate([tot, part_mine], axis=1),
        (lambda: products(0, ex), empty_squares, lambda: None),
    )
    row = 1.0 / total[:, :ROWS]
    partition = total[:, ROWS:]

    def last_sweep(i, acc):
        rows = pl.ds(pl.multiple_of(i * BLK, BLK), BLK)
        k_blk = kt[rows, :]
        col = 1.0 / jnp.sum(k_blk * row, axis=1, keepdims=True)
        k_blk = k_blk * col
        kt[rows, :] = k_blk
        return acc[0] + fold8(k_blk), acc[1] + fold8(k_blk * lg[rows, :])

    acc_k, acc_l = lax.fori_loop(0, COLS // BLK, last_sweep, (zero8, zero8))

    core_copy = remote(pt.at[1 - c], core_in, s_core, r_core, partner)

    def copy_ra(h, j):
        run = run4(h, j)
        dst = (in_a0, in_a1)[h]
        dev = y_peer(j) if h == 0 else x_peer(j)
        return remote(summed.at[run], dst.at[j - 1], s_ra.at[h, j - 1], r_ra.at[h, j - 1], dev)

    def copy_rb(h, j):
        src = (half0, half1)[h]
        dst = (in_b0, in_b1)[h]
        dev = x_peer(j) if h == 0 else y_peer(j)
        spot = lax.rem((x if h == 0 else y) + j, 4)
        return remote(src.at[spot], dst.at[j - 1], s_rb.at[h, j - 1], r_rb.at[h, j - 1], dev)

    def copy_rz(h):
        away = lax.rem(x + 4 * h - z + 8, 8)
        slot = jnp.maximum(away - 1, 0)
        return remote(
            quart.at[h], in_z.at[slot], s_rz.at[h], r_rz.at[slot], at(x, y, x + 4 * h, c)
        )

    def teacher_products():
        products(1, kt)
        core_copy.start()

    def core_sum():
        core_copy.wait_recv()

        @pl.loop(0, 32)
        def _(s):
            summed[s] = (pt[c, s].astype(F32) + core_in[s].astype(F32)).astype(BF16)

        for j in range(1, 4):
            copy_ra(0, j).start()
            copy_ra(1, j).start()

    total = all_sum(
        2, jnp.concatenate([fold1(acc_k), fold1(acc_l)], axis=1),
        (teacher_products, core_sum, lambda: None),
    )
    row = 1.0 / total[:, :ROWS]
    row_w = jnp.concatenate([jnp.full((1, 128), w, F32) for w in ROW_W], axis=1)
    loss = jnp.sum(
        row_w * (jnp.log(partition) - row * total[:, ROWS:]), axis=1, keepdims=True
    )
    loss_ref[...] = loss
    lead = row_w * (ROWS / STUDENT_TEMP)
    scale_p = lead / partition
    scale_t = lead * row
    for kp in range(10):
        scale[0, kp] = scale_p[:, 128 * kp:128 * kp + 128]
        scale[1, kp] = -scale_t[:, 128 * kp:128 * kp + 128]
    scale[0, 10] = jnp.zeros((1, 128), F32)
    scale[1, 10] = jnp.zeros((1, 128), F32)

    for h in range(2):
        for j in range(1, 4):
            copy_ra(h, j).wait_recv()
        own = run4(h, 0)
        got = (in_a0, in_a1)[h]
        v = summed[own].astype(F32)
        for j in range(3):
            v = v + got[j].astype(F32)
        (half0, half1)[h][...] = v.astype(BF16)
        for j in range(1, 4):
            copy_rb(h, j).start()

    @pl.loop(0, COLS // BLK)
    def _(i):
        rows = pl.ds(pl.multiple_of(i * BLK, BLK), BLK)
        gb[rows, :] = (ex[rows, :] * scale_p - kt[rows, :] * scale_t).astype(BF16)

    for h in range(2):
        for j in range(1, 4):
            copy_rb(h, j).wait_recv()
        own = x if h == 0 else y
        got = (in_b0, in_b1)[h]
        v = (half0, half1)[h][own].astype(F32)
        for j in range(3):
            v = v + got[j].astype(F32)
        quart[h] = v.astype(BF16)

        @pl.when(z != x + 4 * h)
        def _():
            copy_rz(h).start()

    gu = dot(gb[...], stu[...]).T
    w_f = w_unit[...].astype(F32)
    gw_ref[...] = (
        1024.0 * (gu - w_f * jnp.sum(w_f * gu, axis=0, keepdims=True)) / w_norm[...]
    )

    sends_back = is_owner & (o_me < 30)

    def copy_back(i):
        return remote(
            tiles.at[i], back.at[k_me, f_me, c], s_back.at[i], r_back, (i, b_me)
        )

    @pl.when(is_owner)
    def _():
        for j in range(1, 8):
            remote(quart.at[0], in_z.at[j - 1], s_rz.at[0], r_rz.at[j - 1], partner).wait_recv()

    @pl.when(sends_back)
    def _():
        v = quart[h_me].astype(F32)
        for j in range(7):
            v = v + in_z[j].astype(F32)
        v = (v * scale[c, kp_me]).T
        t = jnp.dot(sel[...], v, precision=lax.Precision.HIGHEST, preferred_element_type=F32)
        tiles[...] = t.reshape(64, 16, 128)

        @pl.loop(0, 64)
        def _(i):
            mine = (i == img) & (b_me == y)

            @pl.when(jnp.logical_not(mine))
            def _():
                copy_back(i).start()

            @pl.when(mine)
            def _():
                pltpu.make_async_copy(tiles.at[i], back.at[k_me, f_me, c], r_back).start()

    for b in range(4):
        @pl.when(y == b)
        def _():
            got = back.at[pl.ds(0, 4 - b)]
            pltpu.make_async_copy(got, got, r_back).wait()
            for k in range(4 - b, 4):
                back[k] = jnp.zeros((3, 2, 16, 128), F32)

    cols = []
    for f in range(3):
        v = back[0, f, 0]
        for k in range(4):
            for kind in range(2):
                if k or kind:
                    v = v + back[k, f, kind]
        cols.append(v)
    gx = jnp.concatenate(cols, axis=1)
    u = unit_f[y]
    gr_ref[...] = (gx - u * jnp.sum(u * gx, axis=1, keepdims=True)) / norm_f[y][:, :1]

    each_owner(raw_done, None)

    @pl.when(is_owner)
    def _():
        for j in range(1, 8):
            z_copy(j).wait_send()

    for h in range(2):
        for j in range(1, 4):
            copy2(h, j).wait_send()
            copy3(h, j).wait_send()
            copy_ra(h, j).wait_send()
            copy_rb(h, j).wait_send()
        for j in range(4):
            copy_ex(h, j, c).wait_send()

        @pl.when(z != x + 4 * h)
        def _():
            copy_rz(h).wait_send()

    for it in range(3):
        all_sum_sent(it)
    core_copy.wait_send()

    @pl.when(sends_back)
    def _():
        @pl.loop(0, 64)
        def _(i):
            @pl.when(jnp.logical_not((i == img) & (b_me == y)))
            def _():
                copy_back(i).wait_send()


def shards(student_feats, teacher_feats, student_weight, teacher_weight, patch_masks):
    vmem = pl.BlockSpec(memory_space=pltpu.VMEM)
    dma = pltpu.SemaphoreType.DMA

    def sums(width):
        return [pltpu.VMEM((n, 1, width), F32) for n in (8, 4, 8)]

    scratch = [
        pltpu.VMEM((2, 4, 3, 16, 128), BF16),
        pltpu.VMEM((4, 16, E), F32),
        pltpu.VMEM((4, 16, 128), F32),
        pltpu.VMEM((1, 128), F32),
        pltpu.VMEM((64, 16, 128), BF16),
        pltpu.VMEM((64, 1, 128), F32),
        pltpu.VMEM((1024, 128), F32),
        pltpu.VMEM((2, 32, 128, 128), BF16),
        pltpu.VMEM((ROWS, E), BF16),
        pltpu.VMEM((ROWS, E), BF16),
        pltpu.VMEM((E, COLS), BF16),
        pltpu.VMEM((COLS, E), BF16),
        pltpu.VMEM((COLS, E), BF16),
        pltpu.VMEM((1, COLS), F32),
        pltpu.VMEM((COLS, ROWS), F32),
        pltpu.VMEM((COLS, ROWS), F32),
        pltpu.VMEM((COLS, ROWS), F32),
        pltpu.VMEM((COLS, ROWS), BF16),
        pltpu.VMEM((COLS, 128), F32),
        *sums(ROWS), *sums(2 * ROWS), *sums(2 * ROWS),
        pltpu.VMEM((2, 32, 128, 128), BF16),
        pltpu.VMEM((32, 128, 128), BF16),
        pltpu.VMEM((32, 128, 128), BF16),
        pltpu.VMEM((3, 4, 128, 128), BF16),
        pltpu.VMEM((3, 4, 128, 128), BF16),
        pltpu.VMEM((4, 128, 128), BF16),
        pltpu.VMEM((4, 128, 128), BF16),
        pltpu.VMEM((3, 128, 128), BF16),
        pltpu.VMEM((3, 128, 128), BF16),
        pltpu.VMEM((2, 128, 128), BF16),
        pltpu.VMEM((7, 128, 128), BF16),
        pltpu.VMEM((2, 11, 1, 128), F32),
        pltpu.VMEM((64, 16, 128), F32),
        pltpu.VMEM((4, 3, 2, 16, 128), F32),
        dma((16,)), dma((16,)), dma, dma,
        dma((7,)), dma((2,)),
        dma((2, 3)), dma((2, 3)), dma((2, 3)), dma((2, 3)), dma((2, 4)), dma((2, 4)),
        dma((3, 17)), dma((3, 17)),
        dma, dma,
        dma((2, 3)), dma((2, 3)), dma((2, 3)), dma((2, 3)), dma((2,)), dma((7,)),
        dma((64,)), dma,
    ]
    loss, grad_weight, grad_rows = pl.pallas_call(
        kernel,
        out_shape=(
            jax.ShapeDtypeStruct((1, 1), F32),
            jax.ShapeDtypeStruct((E, COLS), F32),
            jax.ShapeDtypeStruct((16, E), F32),
        ),
        in_specs=[vmem] * 5,
        out_specs=(vmem, vmem, vmem),
        scratch_shapes=scratch,
        compiler_params=pltpu.CompilerParams(collective_id=0, has_side_effects=True),
    )(student_feats, teacher_feats, student_weight, teacher_weight, patch_masks)
    return loss.reshape(()), grad_weight, grad_rows


def solution(mesh):
    placed = (
        P("img", None, None),
        P("img", None, None),
        P(None, ("img", "proto")),
        P(None, ("img", "proto")),
        P("img", None),
    )
    return jax.shard_map(
        shards,
        mesh=mesh,
        in_specs=placed,
        out_specs=(P(), P(None, ("img", "proto")), P(("img", "proto"), None)),
        check_vma=False,
    )
```

time: 853 us -> 107 us (0.13)
  blocking collectives: 427 us -> 0 us
  waiting for transfers between devices: 316 us -> 0 us
  Pallas kernels: 0 us -> 101 us
  matrix products: 62 us -> 0 us
  other arithmetic: 19 us -> 0 us
  between operations: 15 us -> 2.41 us
    psum x4 -> x0, blocking collectives: 316 us -> none  [the longest x2 168 us: summed_mass(): return lax.psum(row_part, ('img', 'proto'))]
    reduce_scatter x1 -> x0, waiting for transfers between devices: 316 us -> none  [shards(): lax.psum_scatter(grad_unit_x, ('img', 'proto'), scatter_dimension=0, tile...]
    unnamed x1 -> x0, blocking collectives: 111 us -> none
    pallas_call x0 -> x1, Pallas kernels: none -> 101 us  [shards(): pl.pallas_call(kernel, out_shape=(jax.ShapeDtypeStruct((1, 1), F32), jax....]
    dot_general x12 -> x0, matrix products: 62 us -> none  [the longest x3 22.4 us: shards(): jnp.dot(row_scale, kernel, precision=lax.Precision.HIGHEST)]
    convert_element_type x4 -> x0, other arithmetic: 9.13 us -> none  [the longest x1 7.7 us: shards(): grad_logits = (slot_weight[:, None] * rows_total * (probability - targets...]
  transfers between devices with their start and end apart: 3 -> 0, of which waited for: 1 -> 0; matrix products, arithmetic and copies ran while one was open for 7% -> 0% of each run, Pallas kernels for 0% -> 0%
where the time goes in v1:
time: 107 us; the launch traced here: 106 us
  Pallas kernels  101 us (94%)
  local copies, waits for them, and re-layouts  2.68 us (3%)
  between operations  2.41 us (2%)
    pallas_call x1, Pallas kernels, shards(): pl.pallas_call(kernel, out_shape=(jax.ShapeDtypeStruct((1, 1), F32), jax....  101 us
    unnamed x4, local copies, waits for them, and re-layouts  2.68 us

profile of v1, /device:TPU:6, one launch (start us, length us, event | category | flops | bytes accessed | tf_op | source)
XLA Modules:
  0.0 105.7 jit_solution(11190778952967710749)
XLA Ops:
  0.6 100.7 %shard_map.76 = (f32[1,1]{1,0:T(1,128)}, f32[384,512]{1,0:T(8,128)}, f32[16,384]{1,0:T(8,128)}) custom-call(bf16[1,128,384]{2,1,0:T(8,128)(2,1)} %sf.1, bf16[1,128,384]{2,1,0:T(8,128)(2,1)} %tf.1, bf16[384,512]{1,0:T(8,128)(2,1)} %sw.1, bf16[384,512]{1,0:T(8,128)(2,1)} %tw.1, s32[1,128]{1,0:T(1,128)} %mask.1), custom_call_target="tpu_custom_call" | custom-call | tf_op jit(solution)/shard_map/pallas_call | solution.py:610
  101.9 0.0 copy-start
  101.9 2.1 %copy.12 = f32[384,512]{1,0:T(8,128)} copy(f32[384,512]{1,0:T(8,128)} %get-tuple-element.13) | data formatting | bytes 1572864
  104.0 0.0 copy-done
  104.0 0.6 copy.13
Async XLA Ops:
  101.9 2.1 %copy-start = (f32[16,384]{1,0:T(8,128)S(1)}, f32[16,384]{1,0:T(8,128)}, u32[]{:S(2)}) copy-start(f32[16,384]{1,0:T(8,128)} %get-tuple-element.14) | copy-start | bytes 73732

commit v2 on v1

--- a/solution.py
+++ b/solution.py
@@ -11,7 +11,7 @@
 STUDENT_TEMP = 0.1
 NORM_EPS = 1e-06
 ROWS, COLS, E, ITERS = 1280, 512, 384, 3
-BLK = 64
+BLK = 128
 GROUPS = [(b, m) for b in range(4) for m in range(b + 1, 5)]
 ROW_W = [1.0 / (16.0 * m * 32.0) for _, m in GROUPS]
 
@@ -41,15 +41,16 @@
 
 
 def kernel(
-    sf, tf, sw, tw, mask,
-    loss_ref, gw_ref, gr_ref,
+    sf_hbm, tf_hbm, sw_hbm, tw_hbm, mask_hbm,
+    loss_hbm, gw_ref, gr_ref,
+    sf, tf, sw, tw, mask, loss_ref,
     units, unit_f, norm_f, cnt, raw, rawc, sel, grid, tea, stu,
     w_unit, w_t, tw_t, w_norm, kt, lg, ex, gb, csum,
-    a0, b0, c0, a1, b1, c1, a2, b2, c2,
+    ar_v, ar_a, ar_b, ls_a, ls_b,
     pt, core_in, summed, in_a0, in_a1, half0, half1, in_b0, in_b1, quart, in_z,
-    scale, tiles, back,
+    scale, whole, tiles, back,
     s_raw, s_cnt, r_raw, r_cnt, s_z, r_z, s_2, r_2, s_3, r_3, s_ex, r_ex,
-    s_ar, r_ar, s_core, r_core, s_ra, r_ra, s_rb, r_rb, s_rz, r_rz, s_back, r_back,
+    s_ara, r_ara, s_arb, r_arb, s_lsa, r_lsa, s_lsb, r_lsb, s_core, r_core, s_ra, r_ra, s_rb, r_rb, s_rz, r_rz, s_pair, r_pair, s_back, r_back, s_in, s_loss,
 ):
     img = lax.axis_index("img")
     y = lax.axis_index("proto")
@@ -73,9 +74,19 @@
     def z_peer(j):
         return at(x, y, lax.rem(z + j, 8), c)
 
-    def cy_peer(j):
-        g = lax.rem(c * 4 + y + j, 8)
-        return at(x, lax.rem(g, 4), z, lax.div(g, 4))
+    zc, xy = z * 2 + c, x * 4 + y
+
+    def zc_peer(j):
+        g = lax.rem(zc + j, 16)
+        return at(x, y, lax.div(g, 2), lax.rem(g, 2)), lax.rem(g, 2)
+
+    def xyc_peer(j):
+        g = lax.rem(xy * 2 + c + j, 32)
+        return at(lax.div(g, 8), lax.rem(lax.div(g, 2), 4), z, lax.rem(g, 2))
+
+    def xy_peer(j):
+        g = lax.rem(xy + j, 16)
+        return at(lax.div(g, 4), lax.rem(g, 4), z, c)
 
     partner = at(x, y, z, 1 - c)
 
@@ -84,25 +95,35 @@
             src_ref=src, dst_ref=dst, send_sem=s, recv_sem=r, device_id=dev, device_id_type=MESH
         )
 
+    loads = [
+        pltpu.make_async_copy(src, dst, s_in.at[n])
+        for n, (src, dst) in enumerate(
+            ((mask_hbm, mask), (tf_hbm, tf), (sf_hbm, sf), (tw_hbm, tw), (sw_hbm, sw))
+        )
+    ]
+    for load in loads:
+        load.start()
+
     bar = pltpu.get_barrier_semaphore()
 
     def greet(dev):
         pl.semaphore_signal(bar, inc=1, device_id=dev, device_id_type=MESH)
 
-    for j in range(1, 4):
-        greet(x_peer(j))
-    for j in range(1, 8):
-        greet(z_peer(j))
-        greet(cy_peer(j))
-
     @pl.when(is_owner)
     def _():
-        @pl.loop(0, 64)
+        @pl.loop(0, 63)
         def _(i):
-            @pl.when(i != img)
-            def _():
-                greet((i, y))
-
+            n = lax.rem(i + 24, 63) + 1
+            greet((lax.rem(img + n, 64), y))
+
+    for j in range(1, 16):
+        greet(zc_peer(j)[0])
+    for j in range(1, 32):
+        greet(xyc_peer(j))
+
+
+    for load in loads[:3]:
+        load.wait()
     mrow = mask[...].astype(F32)
     upper = (
         lax.broadcasted_iota(jnp.int32, (128, 128), 0) <= lax.broadcasted_iota(jnp.int32, (128, 128), 1)
@@ -133,11 +154,11 @@
 
     @pl.when(is_owner)
     def _():
-        pl.semaphore_wait(bar, 17 + 15)
+        pl.semaphore_wait(bar, 46 + 15)
 
     @pl.when(jnp.logical_not(is_owner))
     def _():
-        pl.semaphore_wait(bar, 17 + 16)
+        pl.semaphore_wait(bar, 46 + 16)
 
     def each_owner(remote_fn, local_fn):
         for h in range(2):
@@ -181,8 +202,10 @@
         norm = jnp.sqrt(jnp.sum(w * w, axis=0, keepdims=True) + NORM_EPS)
         return w / norm, norm
 
+    loads[3].wait()
     tw_u, _ = unit_columns(tw)
     tw_t[...] = tw_u.T.astype(BF16)
+    loads[4].wait()
     sw_u, sw_n = unit_columns(sw)
     w_norm[...] = sw_n
     w_unit[...] = sw_u.astype(BF16)
@@ -213,7 +236,9 @@
             == lax.bitwise_and(lax.broadcasted_iota(jnp.int32, (1024, 128), 1), 15)
         )
         sel_f = jnp.where(same_row, dot(spread, block_sel), 0.0)
-        sel[...] = sel_f
+        by_core = sel_f.astype(BF16).reshape(32, 2, 16, 128)
+        for core in range(2):
+            sel[core] = by_core[:, core].reshape(512, 128)
         sel_t = sel_f.T.astype(BF16)
         pltpu.make_async_copy(raw, raw, r_raw).wait()
         grid[c, s_me] = dot(sel_t, raw[...].reshape(1024, 128)).astype(BF16)
@@ -248,29 +273,50 @@
         run = run4(h, (4 - j) % 4)
         return remote(grid.at[kind, run], grid.at[kind, run], s_ex.at[h, j], r_ex.at[h, j], partner)
 
-    for j in range(1, 4):
-        copy2(0, j).start()
-        copy2(1, j).start()
-    for h in range(2):
+    def spread_lines():
         for j in range(1, 4):
-            copy2(h, j, 4 - j).wait_recv()
+            copy2(0, j).start()
+            copy2(1, j).start()
+
+    def spread_planes(kind):
+        for h in range(2):
+            for j in range(1, 4):
+                copy2(h, j, 4 - j).wait_recv()
+            for j in range(1, 4):
+                copy3(h, j).start()
+        copy_ex(0, 0, kind).start()
+        copy_ex(1, 0, kind).start()
+
+    def hand_over(kind):
         for j in range(1, 4):
-            copy3(h, j).start()
-    copy_ex(0, 0, c).start()
-    copy_ex(1, 0, c).start()
-    for j in range(1, 4):
-        for h in range(2):
-            copy3(h, j, 4 - j).wait_recv()
-            copy_ex(h, j, c).start()
-    for h in range(2):
-        for j in range(4):
-            copy_ex(h, j, 1 - c).wait_recv()
-
-    for kind, feats in ((1, tea), (0, stu)):
+            for h in range(2):
+                copy3(h, j, 4 - j).wait_recv()
+                copy_ex(h, j, kind).start()
+
+    def take_over(kind, js):
+        for j in js:
+            for h in range(2):
+                copy_ex(h, j, kind).wait_recv()
+
+    def assemble(kind, feats):
         for s in range(30):
             o = square_at(s)
             kp, f = o // 3, o % 3
             feats[128 * kp:128 * kp + 128, 128 * f:128 * f + 128] = grid[kind, s]
+
+    @pl.when(c == 1)
+    def _():
+        spread_lines()
+        spread_planes(1)
+        hand_over(1)
+
+    @pl.when(c == 0)
+    def _():
+        take_over(1, (0, 1))
+        spread_lines()
+        take_over(1, (2, 3))
+
+    assemble(1, tea)
 
     for n in range(5):
         cols = slice(256 * n, 256 * n + 256)
@@ -290,35 +336,118 @@
 
     tot = fold1(lax.fori_loop(0, COLS // BLK, first_sweep, zero8))
 
-    stages = ((a0, b0, c0), (a1, b1, c1), (a2, b2, c2))
-    spots = (c * 4 + y, x, z)
-    sizes = (8, 4, 8)
-    sem_at = (0, 7, 10)
-
-    def ar_copy(it, st, j):
-        ref = stages[it][st]
-        peer = (cy_peer, x_peer, z_peer)[st](j)
-        n = sem_at[st] + j - 1
-        return remote(ref.at[spots[st]], ref.at[spots[st]], s_ar.at[it, n], r_ar.at[it, n], peer)
-
-    def all_sum(it, v, fillers):
-        for st in range(3):
-            ref = stages[it][st]
-            ref[spots[st]] = v
-            for j in range(1, sizes[st]):
-                ar_copy(it, st, j).start()
-            fillers[st]()
-            for j in range(1, sizes[st]):
-                ar_copy(it, st, j).wait_recv()
-            v = ref[0]
-            for k in range(1, sizes[st]):
-                v = v + ref[k]
-        return v
-
-    def all_sum_sent(it):
-        for st in range(3):
-            for j in range(1, sizes[st]):
-                ar_copy(it, st, j).wait_send()
+    def ar_a_copy(k, j):
+        dev, half = zc_peer(j)
+        return remote(ar_v.at[k, half], ar_a.at[k, zc], s_ara.at[k], r_ara.at[k], dev)
+
+    def ar_b_copy(k, j):
+        ref = ar_b.at[k, c * 16 + xy]
+        return remote(ref, ref, s_arb.at[k], r_arb.at[k], xyc_peer(j))
+
+    def wait_bytes(ref, sem):
+        pltpu.make_async_copy(ref, ref, sem).wait()
+
+    def sum_start(k, v):
+        ar_v[k, 0] = v[:, :640]
+        ar_v[k, 1] = v[:, 640:]
+        for j in range(1, 16):
+            ar_a_copy(k, j).start()
+        ar_a[k, zc] = ar_v[k, c]
+
+    def sum_turn(k):
+        wait_bytes(ar_a.at[k, pl.ds(0, 15)], r_ara.at[k])
+        v = ar_a[k, 0]
+        for i in range(1, 16):
+            v = v + ar_a[k, i]
+        ar_b[k, c * 16 + xy] = v
+        for j in range(1, 32):
+            ar_b_copy(k, j).start()
+
+    def sum_end(k):
+        wait_bytes(ar_b.at[k, pl.ds(0, 31)], r_arb.at[k])
+        halves = []
+        for half in range(2):
+            v = ar_b[k, half * 16]
+            for i in range(1, 16):
+                v = v + ar_b[k, half * 16 + i]
+            halves.append(v)
+        return jnp.concatenate(halves, axis=1)
+
+    def sum_sent(k):
+        wait_bytes(ar_a.at[k, pl.ds(0, 15)], s_ara.at[k])
+        wait_bytes(ar_b.at[k, pl.ds(0, 31)], s_arb.at[k])
+
+    core_copy = remote(pt.at[1 - c], core_in, s_core, r_core, partner)
+
+    def copy_ra(h, j):
+        run = run4(h, j)
+        dst = (in_a0, in_a1)[h]
+        dev = y_peer(j) if h == 0 else x_peer(j)
+        return remote(summed.at[run], dst.at[j - 1], s_ra.at[h, j - 1], r_ra.at[h, j - 1], dev)
+
+    def copy_rb(h, j):
+        src = (half0, half1)[h]
+        dst = (in_b0, in_b1)[h]
+        dev = x_peer(j) if h == 0 else y_peer(j)
+        spot = lax.rem((x if h == 0 else y) + j, 4)
+        return remote(src.at[spot], dst.at[j - 1], s_rb.at[h, j - 1], r_rb.at[h, j - 1], dev)
+
+    def copy_rz(h):
+        away = lax.rem(x + 4 * h - z + 8, 8)
+        slot = jnp.maximum(away - 1, 0)
+        return remote(
+            quart.at[h], in_z.at[slot], s_rz.at[h], r_rz.at[slot], at(x, y, x + 4 * h, c)
+        )
+
+    def core_sum():
+        core_copy.wait_recv()
+
+        @pl.loop(0, 32)
+        def _(s):
+            summed[s] = (pt[c, s].astype(F32) + core_in[s].astype(F32)).astype(BF16)
+
+        for j in range(1, 4):
+            copy_ra(0, j).start()
+            copy_ra(1, j).start()
+
+    def line_sums():
+        for h in range(2):
+            for j in range(1, 4):
+                copy_ra(h, j).wait_recv()
+            own = run4(h, 0)
+            got = (in_a0, in_a1)[h]
+            v = summed[own].astype(F32)
+            for j in range(3):
+                v = v + got[j].astype(F32)
+            (half0, half1)[h][...] = v.astype(BF16)
+            for j in range(1, 4):
+                copy_rb(h, j).start()
+
+    def plane_sums():
+        for h in range(2):
+            for j in range(1, 4):
+                copy_rb(h, j).wait_recv()
+            own = x if h == 0 else y
+            got = (in_b0, in_b1)[h]
+            v = (half0, half1)[h][own].astype(F32)
+            for j in range(3):
+                v = v + got[j].astype(F32)
+            quart[h] = v
+
+            @pl.when(z != x + 4 * h)
+            def _():
+                copy_rz(h).start()
+
+    pair_copy = remote(whole.at[c], whole.at[c], s_pair, r_pair, partner)
+
+    def finish_square():
+        for j in range(1, 8):
+            remote(quart.at[0], in_z.at[j - 1], s_rz.at[0], r_rz.at[j - 1], partner).wait_recv()
+        v = quart[h_me]
+        for j in range(7):
+            v = v + in_z[j]
+        whole[c] = v * scale[c, kp_me]
+        pair_copy.start()
 
     parts = []
 
@@ -342,10 +471,38 @@
                     lo = 128 * (kp % 2)
                     pt[kind, s] = p_blk[128 * f:128 * f + 128, lo:lo + 128]
 
-    total = all_sum(
-        0, tot, (lambda: student((0, 1)), lambda: student((2,)), lambda: student((3, 4)))
-    )
-    row = 1.0 / total
+    def empty_squares():
+        for kind in range(2):
+            for s in (30, 31):
+                pt[kind, s] = jnp.zeros((128, 128), BF16)
+
+    sum_start(0, tot)
+
+    @pl.when(c == 0)
+    def _():
+        spread_planes(0)
+
+    sum_turn(0)
+
+    @pl.when(c == 0)
+    def _():
+        hand_over(0)
+
+    @pl.when(c == 1)
+    def _():
+        take_over(0, range(4))
+
+    assemble(0, stu)
+    student(range(5))
+    sum_start(3, jnp.concatenate(parts, axis=1))
+    products(0, ex)
+    empty_squares()
+
+    @pl.when(c == 1)
+    def _():
+        core_copy.start()
+
+    row = 1.0 / sum_end(0)
 
     def sweep(i, acc):
         rows = pl.ds(pl.multiple_of(i * BLK, BLK), BLK)
@@ -354,19 +511,14 @@
         return acc + fold8(k_blk * col)
 
     tot = fold1(lax.fori_loop(0, COLS // BLK, sweep, zero8))
-    part_mine = jnp.concatenate(parts, axis=1)
-
-    def empty_squares():
-        for kind in range(2):
-            for s in (30, 31):
-                pt[kind, s] = jnp.zeros((128, 128), BF16)
-
-    total = all_sum(
-        1, jnp.concatenate([tot, part_mine], axis=1),
-        (lambda: products(0, ex), empty_squares, lambda: None),
-    )
-    row = 1.0 / total[:, :ROWS]
-    partition = total[:, ROWS:]
+    sum_start(1, tot)
+
+    @pl.when(c == 0)
+    def _():
+        core_sum()
+
+    sum_turn(1)
+    row = 1.0 / sum_end(1)
 
     def last_sweep(i, acc):
         rows = pl.ds(pl.multiple_of(i * BLK, BLK), BLK)
@@ -378,53 +530,44 @@
 
     acc_k, acc_l = lax.fori_loop(0, COLS // BLK, last_sweep, (zero8, zero8))
 
-    core_copy = remote(pt.at[1 - c], core_in, s_core, r_core, partner)
-
-    def copy_ra(h, j):
-        run = run4(h, j)
-        dst = (in_a0, in_a1)[h]
-        dev = y_peer(j) if h == 0 else x_peer(j)
-        return remote(summed.at[run], dst.at[j - 1], s_ra.at[h, j - 1], r_ra.at[h, j - 1], dev)
-
-    def copy_rb(h, j):
-        src = (half0, half1)[h]
-        dst = (in_b0, in_b1)[h]
-        dev = x_peer(j) if h == 0 else y_peer(j)
-        spot = lax.rem((x if h == 0 else y) + j, 4)
-        return remote(src.at[spot], dst.at[j - 1], s_rb.at[h, j - 1], r_rb.at[h, j - 1], dev)
-
-    def copy_rz(h):
-        away = lax.rem(x + 4 * h - z + 8, 8)
-        slot = jnp.maximum(away - 1, 0)
-        return remote(
-            quart.at[h], in_z.at[slot], s_rz.at[h], r_rz.at[slot], at(x, y, x + 4 * h, c)
-        )
-
-    def teacher_products():
-        products(1, kt)
+    sum_start(2, fold1(acc_k))
+    sum_turn(3)
+    products(1, kt)
+
+    @pl.when(c == 0)
+    def _():
         core_copy.start()
-
-    def core_sum():
-        core_copy.wait_recv()
-
-        @pl.loop(0, 32)
-        def _(s):
-            summed[s] = (pt[c, s].astype(F32) + core_in[s].astype(F32)).astype(BF16)
-
-        for j in range(1, 4):
-            copy_ra(0, j).start()
-            copy_ra(1, j).start()
-
-    total = all_sum(
-        2, jnp.concatenate([fold1(acc_k), fold1(acc_l)], axis=1),
-        (teacher_products, core_sum, lambda: None),
-    )
-    row = 1.0 / total[:, :ROWS]
+        line_sums()
+
+    @pl.when(c == 1)
+    def _():
+        core_sum()
+
+    sum_turn(2)
+    partition = sum_end(3)
+
+    @pl.when(c == 0)
+    def _():
+        plane_sums()
+
+    @pl.when(c == 1)
+    def _():
+        line_sums()
+
+    row = 1.0 / sum_end(2)
     row_w = jnp.concatenate([jnp.full((1, 128), w, F32) for w in ROW_W], axis=1)
-    loss = jnp.sum(
-        row_w * (jnp.log(partition) - row * total[:, ROWS:]), axis=1, keepdims=True
-    )
-    loss_ref[...] = loss
+    log_term = jnp.sum(row_w * jnp.log(partition), axis=1, keepdims=True)
+    cross = jnp.sum(row_w * row * fold1(acc_l), axis=1, keepdims=True)
+    ls_a[zc] = jnp.broadcast_to(cross, (1, 128))
+
+    def ls_a_copy(j):
+        return remote(ls_a.at[zc], ls_a.at[zc], s_lsa, r_lsa, zc_peer(j)[0])
+
+    def ls_b_copy(j):
+        return remote(ls_b.at[xy], ls_b.at[xy], s_lsb, r_lsb, xy_peer(j))
+
+    for j in range(1, 16):
+        ls_a_copy(j).start()
     lead = row_w * (ROWS / STUDENT_TEMP)
     scale_p = lead / partition
     scale_t = lead * row
@@ -434,75 +577,66 @@
     scale[0, 10] = jnp.zeros((1, 128), F32)
     scale[1, 10] = jnp.zeros((1, 128), F32)
 
-    for h in range(2):
-        for j in range(1, 4):
-            copy_ra(h, j).wait_recv()
-        own = run4(h, 0)
-        got = (in_a0, in_a1)[h]
-        v = summed[own].astype(F32)
-        for j in range(3):
-            v = v + got[j].astype(F32)
-        (half0, half1)[h][...] = v.astype(BF16)
-        for j in range(1, 4):
-            copy_rb(h, j).start()
+    @pl.when(is_owner & (c == 0))
+    def _():
+        finish_square()
 
     @pl.loop(0, COLS // BLK)
     def _(i):
         rows = pl.ds(pl.multiple_of(i * BLK, BLK), BLK)
         gb[rows, :] = (ex[rows, :] * scale_p - kt[rows, :] * scale_t).astype(BF16)
 
-    for h in range(2):
-        for j in range(1, 4):
-            copy_rb(h, j).wait_recv()
-        own = x if h == 0 else y
-        got = (in_b0, in_b1)[h]
-        v = (half0, half1)[h][own].astype(F32)
-        for j in range(3):
-            v = v + got[j].astype(F32)
-        quart[h] = v.astype(BF16)
-
-        @pl.when(z != x + 4 * h)
-        def _():
-            copy_rz(h).start()
+    @pl.when(c == 1)
+    def _():
+        plane_sums()
 
     gu = dot(gb[...], stu[...]).T
     w_f = w_unit[...].astype(F32)
     gw_ref[...] = (
         1024.0 * (gu - w_f * jnp.sum(w_f * gu, axis=0, keepdims=True)) / w_norm[...]
     )
+    wait_bytes(ls_a.at[pl.ds(0, 15)], r_lsa)
+    v = ls_a[0]
+    for i in range(1, 16):
+        v = v + ls_a[i]
+    ls_b[xy] = v
+    for j in range(1, 16):
+        ls_b_copy(j).start()
 
     sends_back = is_owner & (o_me < 30)
 
     def copy_back(i):
         return remote(
-            tiles.at[i], back.at[k_me, f_me, c], s_back.at[i], r_back, (i, b_me)
+            tiles.at[i], back.at[k_me, f_me], s_back.at[i], r_back, (2 * i + c, b_me)
         )
 
+    def stays(i):
+        return (2 * i + c == img) & (b_me == y)
+
+    @pl.when(is_owner & (c == 1))
+    def _():
+        finish_square()
+
     @pl.when(is_owner)
     def _():
-        for j in range(1, 8):
-            remote(quart.at[0], in_z.at[j - 1], s_rz.at[0], r_rz.at[j - 1], partner).wait_recv()
+        remote(whole.at[1 - c], whole.at[1 - c], s_pair, r_pair, partner).wait_recv()
 
     @pl.when(sends_back)
     def _():
-        v = quart[h_me].astype(F32)
-        for j in range(7):
-            v = v + in_z[j].astype(F32)
-        v = (v * scale[c, kp_me]).T
-        t = jnp.dot(sel[...], v, precision=lax.Precision.HIGHEST, preferred_element_type=F32)
-        tiles[...] = t.reshape(64, 16, 128)
-
-        @pl.loop(0, 64)
+        v = (whole[0] + whole[1]).T
+        hi = v.astype(BF16)
+        lo = (v - hi.astype(F32)).astype(BF16)
+        tiles[...] = (dot(sel[c], hi) + dot(sel[c], lo)).reshape(32, 16, 128)
+
+        @pl.loop(0, 32)
         def _(i):
-            mine = (i == img) & (b_me == y)
-
-            @pl.when(jnp.logical_not(mine))
+            @pl.when(jnp.logical_not(stays(i)))
             def _():
                 copy_back(i).start()
 
-            @pl.when(mine)
+            @pl.when(stays(i))
             def _():
-                pltpu.make_async_copy(tiles.at[i], back.at[k_me, f_me, c], r_back).start()
+                pltpu.make_async_copy(tiles.at[i], back.at[k_me, f_me], r_back).start()
 
     for b in range(4):
         @pl.when(y == b)
@@ -510,24 +644,28 @@
             got = back.at[pl.ds(0, 4 - b)]
             pltpu.make_async_copy(got, got, r_back).wait()
             for k in range(4 - b, 4):
-                back[k] = jnp.zeros((3, 2, 16, 128), F32)
+                back[k] = jnp.zeros((3, 16, 128), F32)
 
     cols = []
     for f in range(3):
-        v = back[0, f, 0]
-        for k in range(4):
-            for kind in range(2):
-                if k or kind:
-                    v = v + back[k, f, kind]
-        cols.append(v)
+        cols.append(back[0, f] + back[1, f] + back[2, f] + back[3, f])
     gx = jnp.concatenate(cols, axis=1)
     u = unit_f[y]
     gr_ref[...] = (gx - u * jnp.sum(u * gx, axis=1, keepdims=True)) / norm_f[y][:, :1]
 
+    wait_bytes(ls_b.at[pl.ds(0, 15)], r_lsb)
+    v = ls_b[0]
+    for i in range(1, 16):
+        v = v + ls_b[i]
+    loss_ref[...] = log_term - v[:, :1]
+    store_loss = pltpu.make_async_copy(loss_ref, loss_hbm, s_loss)
+    store_loss.start()
+
     each_owner(raw_done, None)
 
     @pl.when(is_owner)
     def _():
+        pair_copy.wait_send()
         for j in range(1, 8):
             z_copy(j).wait_send()
 
@@ -544,34 +682,41 @@
         def _():
             copy_rz(h).wait_send()
 
-    for it in range(3):
-        all_sum_sent(it)
+    for k in range(4):
+        sum_sent(k)
+    wait_bytes(ls_a.at[pl.ds(0, 15)], s_lsa)
+    wait_bytes(ls_b.at[pl.ds(0, 15)], s_lsb)
+    store_loss.wait()
     core_copy.wait_send()
 
     @pl.when(sends_back)
     def _():
-        @pl.loop(0, 64)
+        @pl.loop(0, 32)
         def _(i):
-            @pl.when(jnp.logical_not((i == img) & (b_me == y)))
+            @pl.when(jnp.logical_not(stays(i)))
             def _():
                 copy_back(i).wait_send()
 
 
 def shards(student_feats, teacher_feats, student_weight, teacher_weight, patch_masks):
     vmem = pl.BlockSpec(memory_space=pltpu.VMEM)
+    hbm = pl.BlockSpec(memory_space=pltpu.HBM)
     dma = pltpu.SemaphoreType.DMA
 
-    def sums(width):
-        return [pltpu.VMEM((n, 1, width), F32) for n in (8, 4, 8)]
-
     scratch = [
+        pltpu.VMEM((1, 128, E), BF16),
+        pltpu.VMEM((1, 128, E), BF16),
+        pltpu.VMEM((E, COLS), BF16),
+        pltpu.VMEM((E, COLS), BF16),
+        pltpu.VMEM((1, 128), jnp.int32),
+        pltpu.VMEM((1, 1), F32),
         pltpu.VMEM((2, 4, 3, 16, 128), BF16),
         pltpu.VMEM((4, 16, E), F32),
         pltpu.VMEM((4, 16, 128), F32),
         pltpu.VMEM((1, 128), F32),
         pltpu.VMEM((64, 16, 128), BF16),
         pltpu.VMEM((64, 1, 128), F32),
-        pltpu.VMEM((1024, 128), F32),
+        pltpu.VMEM((2, 512, 128), BF16),
         pltpu.VMEM((2, 32, 128, 128), BF16),
         pltpu.VMEM((ROWS, E), BF16),
         pltpu.VMEM((ROWS, E), BF16),
@@ -584,7 +729,11 @@
         pltpu.VMEM((COLS, ROWS), F32),
         pltpu.VMEM((COLS, ROWS), BF16),
         pltpu.VMEM((COLS, 128), F32),
-        *sums(ROWS), *sums(2 * ROWS), *sums(2 * ROWS),
+        pltpu.VMEM((4, 2, 1, 640), F32),
+        pltpu.VMEM((4, 16, 1, 640), F32),
+        pltpu.VMEM((4, 32, 1, 640), F32),
+        pltpu.VMEM((16, 1, 128), F32),
+        pltpu.VMEM((16, 1, 128), F32),
         pltpu.VMEM((2, 32, 128, 128), BF16),
         pltpu.VMEM((32, 128, 128), BF16),
         pltpu.VMEM((32, 128, 128), BF16),
@@ -594,18 +743,21 @@
         pltpu.VMEM((4, 128, 128), BF16),
         pltpu.VMEM((3, 128, 128), BF16),
         pltpu.VMEM((3, 128, 128), BF16),
-        pltpu.VMEM((2, 128, 128), BF16),
-        pltpu.VMEM((7, 128, 128), BF16),
+        pltpu.VMEM((2, 128, 128), F32),
+        pltpu.VMEM((7, 128, 128), F32),
         pltpu.VMEM((2, 11, 1, 128), F32),
-        pltpu.VMEM((64, 16, 128), F32),
-        pltpu.VMEM((4, 3, 2, 16, 128), F32),
+        pltpu.VMEM((2, 128, 128), F32),
+        pltpu.VMEM((32, 16, 128), F32),
+        pltpu.VMEM((4, 3, 16, 128), F32),
         dma((16,)), dma((16,)), dma, dma,
         dma((7,)), dma((2,)),
         dma((2, 3)), dma((2, 3)), dma((2, 3)), dma((2, 3)), dma((2, 4)), dma((2, 4)),
-        dma((3, 17)), dma((3, 17)),
+        dma((4,)), dma((4,)), dma((4,)), dma((4,)), dma, dma, dma, dma,
         dma, dma,
         dma((2, 3)), dma((2, 3)), dma((2, 3)), dma((2, 3)), dma((2,)), dma((7,)),
-        dma((64,)), dma,
+        dma, dma,
+        dma((32,)), dma,
+        dma((5,)), dma,
     ]
     loss, grad_weight, grad_rows = pl.pallas_call(
         kernel,
@@ -614,11 +766,16 @@
             jax.ShapeDtypeStruct((E, COLS), F32),
             jax.ShapeDtypeStruct((16, E), F32),
         ),
-        in_specs=[vmem] * 5,
-        out_specs=(vmem, vmem, vmem),
+        in_specs=[hbm] * 5,
+        out_specs=(hbm, vmem, vmem),
         scratch_shapes=scratch,
-        compiler_params=pltpu.CompilerParams(collective_id=0, has_side_effects=True),
-    )(student_feats, teacher_feats, student_weight, teacher_weight, patch_masks)
+        compiler_params=pltpu.CompilerParams(
+            collective_id=0, has_side_effects=True, vmem_limit_bytes=40 * 2**20
+        ),
+    )(*(
+        pltpu.with_memory_space_constraint(a, pltpu.HBM)
+        for a in (student_feats, teacher_feats, student_weight, teacher_weight, patch_masks)
+    ))
     return loss.reshape(()), grad_weight, grad_rows
 
 

time: 107 us -> 91.3 us (0.85)
  Pallas kernels: 101 us -> 85.8 us
  local copies, waits for them, and re-layouts: 2.68 us -> 1.49 us
    pallas_call x1, Pallas kernels: 101 us -> 85.8 us  [shards(): pl.pallas_call(kernel, out_shape=(jax.ShapeDtypeStruct((1, 1), F32), jax....]
    unnamed x4 -> x2, local copies, waits for them, and re-layouts: 2.68 us -> 1.49 us
where the time goes in v2:
time: 91.3 us; the launch traced here: 89.6 us
  Pallas kernels  85.8 us (94%)
  between operations  2.33 us (3%)
  local copies, waits for them, and re-layouts  1.49 us (2%)
    pallas_call x1, Pallas kernels, shards(): pl.pallas_call(kernel, out_shape=(jax.ShapeDtypeStruct((1, 1), F32), jax....  85.8 us

profile of v2, /device:TPU:6, one launch (start us, length us, event | category | flops | bytes accessed | tf_op | source)
XLA Modules:
  0.0 89.6 jit_solution(10588621850238352248)
XLA Ops:
  0.6 85.8 %shard_map.76 = (f32[1,1]{1,0:T(1,128)}, f32[384,512]{1,0:T(8,128)S(1)}, f32[16,384]{1,0:T(8,128)S(1)}) custom-call(bf16[1,128,384]{2,1,0:T(8,128)(2,1)} %sf_hbm.1, bf16[1,128,384]{2,1,0:T(8,128)(2,1)} %tf_hbm.1, bf16[384,512]{1,0:T(8,128)(2,1)} %sw_hbm.1, bf16[384,512]{1,0:T(8,128)(2,1)} %tw_hbm.1, s32[1,128]{1,0:T(1,128)} %mask_hbm.1), custom_call_target="tpu_custom_call" | custom-call | tf_op jit(solution)/shard_map/pallas_call | solution.py:762
  87.0 0.9 copy.12
  87.8 0.6 copy.13

commit v3 on v2

--- a/solution.py
+++ b/solution.py
@@ -17,7 +17,19 @@
 
 
 def square_at(s):
-    return 4 * (s % 4) + s // 4 if s < 16 else s
+    y, q = (s // 4, s % 4) if s < 16 else (s % 4, s // 4)
+    if q == 7 and y >= 2:
+        return 28 + y
+    return q + (0, 12, 20, 8)[y] + (15 if y == 3 and q >= 4 else 0)
+
+
+SPOT_OF = {square_at(s): s for s in range(32)}
+
+
+def square_on(y, q):
+    base = jnp.where(y == 0, 0, jnp.where(y == 1, 12, jnp.where(y == 2, 20, 8)))
+    o = q + base + jnp.where((y == 3) & (q >= 4), 15, 0)
+    return jnp.where((q == 7) & (y >= 2), 28 + y, o)
 
 
 def split_square(o):
@@ -50,7 +62,7 @@
     pt, core_in, summed, in_a0, in_a1, half0, half1, in_b0, in_b1, quart, in_z,
     scale, whole, tiles, back,
     s_raw, s_cnt, r_raw, r_cnt, s_z, r_z, s_2, r_2, s_3, r_3, s_ex, r_ex,
-    s_ara, r_ara, s_arb, r_arb, s_lsa, r_lsa, s_lsb, r_lsb, s_core, r_core, s_ra, r_ra, s_rb, r_rb, s_rz, r_rz, s_pair, r_pair, s_back, r_back, s_in, s_loss,
+    s_ara, r_ara, s_arb, r_arb, s_lsa, r_lsa, s_lsb, r_lsb, s_core, r_core, s_ra, r_ra, s_rb, r_rb, s_rz, r_rz, s_pair, r_pair, s_back, r_back, s_in, s_loss, turn,
 ):
     img = lax.axis_index("img")
     y = lax.axis_index("proto")
@@ -59,8 +71,8 @@
     x = lax.div(img, 16)
     is_owner = lax.rem(z, 4) == x
     h_me = lax.div(z, 4)
-    o_me = 16 * h_me + 4 * x + y
-    s_me = jnp.where(h_me == 0, 4 * y + x, o_me)
+    o_me = square_on(y, 4 * h_me + x)
+    s_me = jnp.where(h_me == 0, 4 * y + x, 16 + 4 * x + y)
 
     def at(px, py, pz, pc):
         return ((px * 8 + pz) * 2 + pc, py)
@@ -109,12 +121,14 @@
     def greet(dev):
         pl.semaphore_signal(bar, inc=1, device_id=dev, device_id_type=MESH)
 
+    def hops(n):
+        px, pz = n // 16, n // 2 % 8
+        return min(px, 4 - px) + min(pz, 8 - pz)
+
     @pl.when(is_owner)
     def _():
-        @pl.loop(0, 63)
-        def _(i):
-            n = lax.rem(i + 24, 63) + 1
-            greet((lax.rem(img + n, 64), y))
+        for n in sorted(range(1, 64), key=hops, reverse=True):
+            greet((lax.bitwise_and(img + n, 63), y))
 
     for j in range(1, 16):
         greet(zc_peer(j)[0])
@@ -160,13 +174,13 @@
     def _():
         pl.semaphore_wait(bar, 46 + 16)
 
-    def each_owner(remote_fn, local_fn):
-        for h in range(2):
-            for px in range(4):
-                for pc in range(2):
+    def each_owner(remote_fn, local_fn, cores=(1, 0)):
+        for pc in cores:
+            for h in range(2):
+                for px in range(4):
                     t = (h * 4 + px) * 2 + pc
                     to = (px * 8 + px + 4 * h) * 2 + pc
-                    _, f, b, _, _ = split_square(16 * h + 4 * px + y)
+                    _, f, b, _, _ = split_square(square_on(y, 4 * h + px))
 
                     @pl.when(img != to)
                     def _():
@@ -177,25 +191,32 @@
                         def _():
                             local_fn(pc, b, f)
 
-    def raw_copies(t, to, pc, b, f):
-        return (
-            remote(cnt, rawc.at[img], s_cnt.at[t], r_cnt, (to, y)),
-            remote(units.at[pc, b, f], raw.at[img], s_raw.at[t], r_raw, (to, y)),
-        )
-
-    def raw_start(*a):
-        for cp in raw_copies(*a):
-            cp.start()
-
-    def raw_done(*a):
-        for cp in raw_copies(*a):
-            cp.wait_send()
-
-    def raw_local(pc, b, f):
+    def cnt_copy(t, to, pc, b, f):
+        return remote(cnt, rawc.at[img], s_cnt.at[t], r_cnt, (to, y))
+
+    def tile_copy(t, to, pc, b, f):
+        return remote(units.at[pc, b, f], raw.at[img], s_raw.at[t], r_raw, (to, y))
+
+    def cnt_start(*a):
+        cnt_copy(*a).start()
+
+    def tile_start(*a):
+        tile_copy(*a).start()
+
+    def cnt_done(*a):
+        cnt_copy(*a).wait_send()
+
+    def tile_done(*a):
+        tile_copy(*a).wait_send()
+
+    def cnt_local(pc, b, f):
         pltpu.make_async_copy(cnt, rawc.at[img], r_cnt).start()
+
+    def tile_local(pc, b, f):
         pltpu.make_async_copy(units.at[pc, b, f], raw.at[img], r_raw).start()
 
-    each_owner(raw_start, raw_local)
+    each_owner(cnt_start, cnt_local)
+    each_owner(tile_start, tile_local, (1,))
 
     def unit_columns(w_ref):
         w = w_ref[...].astype(F32)
@@ -211,6 +232,9 @@
     w_unit[...] = sw_u.astype(BF16)
     w_t[...] = sw_u.T.astype(BF16)
 
+    each_owner(tile_done, None, (1,))
+    each_owner(tile_start, tile_local, (0,))
+
     kp_me, f_me, b_me, k_me, m_me = split_square(o_me)
 
     def z_copy(j):
@@ -225,25 +249,48 @@
             lax.broadcasted_iota(jnp.int32, (64, 64), 1) < lax.broadcasted_iota(jnp.int32, (64, 64), 0)
         ).astype(BF16)
         place = jnp.where(match > 0.5, dot(lower, match.astype(BF16)), -1.0)
+        lane_image = lax.shift_right_logical(lax.broadcasted_iota(jnp.int32, (64, 1024), 1), 4)
+        own_image = lane_image == lax.broadcasted_iota(jnp.int32, (64, 1024), 0)
+        along = jnp.where(own_image, jnp.broadcast_to(place[:, :1], (64, 1024)), 0.0)
+        place_row = dot(jnp.ones((8, 64), BF16), along.astype(BF16))
+        sub = lax.broadcasted_iota(jnp.int32, (128, 1024), 0)
+        same_row = lax.bitwise_and(sub, 15) == lax.bitwise_and(
+            lax.broadcasted_iota(jnp.int32, (128, 1024), 1), 15
+        )
+        slot_block = lax.shift_right_logical(sub, 4).astype(F32)
+        sel_t = jnp.where(
+            same_row & (jnp.broadcast_to(place_row[:1], (128, 1024)) == slot_block), 1.0, 0.0
+        ).astype(BF16)
+        pltpu.make_async_copy(raw, raw, r_raw).wait()
+        grid[c, s_me] = dot(sel_t, raw[...].reshape(1024, 128)).astype(BF16)
+
+        @pl.when(c == 0)
+        def _():
+            pl.semaphore_wait(turn, 1)
+
+        for j in range(1, 8):
+            z_copy(j).start()
+
         lane_block = lax.shift_right_logical(lax.broadcasted_iota(jnp.int32, (64, 128), 1), 4)
         block_sel = jnp.where(place == lane_block.astype(F32), 1.0, 0.0).astype(BF16)
         spread = (
             lax.shift_right_logical(lax.broadcasted_iota(jnp.int32, (1024, 64), 0), 4)
             == lax.broadcasted_iota(jnp.int32, (1024, 64), 1)
         ).astype(BF16)
-        same_row = (
+        same_lane = (
             lax.bitwise_and(lax.broadcasted_iota(jnp.int32, (1024, 128), 0), 15)
             == lax.bitwise_and(lax.broadcasted_iota(jnp.int32, (1024, 128), 1), 15)
         )
-        sel_f = jnp.where(same_row, dot(spread, block_sel), 0.0)
+        sel_f = jnp.where(same_lane, dot(spread, block_sel), 0.0)
         by_core = sel_f.astype(BF16).reshape(32, 2, 16, 128)
         for core in range(2):
             sel[core] = by_core[:, core].reshape(512, 128)
-        sel_t = sel_f.T.astype(BF16)
-        pltpu.make_async_copy(raw, raw, r_raw).wait()
-        grid[c, s_me] = dot(sel_t, raw[...].reshape(1024, 128)).astype(BF16)
-        for j in range(1, 8):
-            z_copy(j).start()
+
+        @pl.when(c == 1)
+        def _():
+            for j in range(1, 8):
+                z_copy(j).wait_send()
+            pl.semaphore_signal(turn, inc=1, device_id=partner, device_id_type=MESH)
 
     for h in range(2):
         spot = 4 * y + x if h == 0 else 16 + 4 * x + y
@@ -299,9 +346,8 @@
                 copy_ex(h, j, kind).wait_recv()
 
     def assemble(kind, feats):
-        for s in range(30):
-            o = square_at(s)
-            kp, f = o // 3, o % 3
+        for o in range(30):
+            s, kp, f = SPOT_OF[o], o // 3, o % 3
             feats[128 * kp:128 * kp + 128, 128 * f:128 * f + 128] = grid[kind, s]
 
     @pl.when(c == 1)
@@ -373,11 +419,49 @@
             halves.append(v)
         return jnp.concatenate(halves, axis=1)
 
+    def late_a_copy(k, j):
+        half = lax.rem(xy * 2 + c + j, 2)
+        return remote(
+            ar_v.at[k, half], ar_b.at[k, xy * 2 + c], s_arb.at[k], r_arb.at[k], xyc_peer(j)
+        )
+
+    def late_b_copy(k, j):
+        ref = ar_a.at[k, c * 8 + z]
+        return remote(ref, ref, s_ara.at[k], r_ara.at[k], zc_peer(j)[0])
+
+    def late_start(k, v):
+        ar_v[k, 0] = v[:, :640]
+        ar_v[k, 1] = v[:, 640:]
+        for j in range(1, 32):
+            late_a_copy(k, j).start()
+        ar_b[k, xy * 2 + c] = ar_v[k, c]
+
+    def late_turn(k):
+        wait_bytes(ar_b.at[k, pl.ds(0, 31)], r_arb.at[k])
+        v = ar_b[k, 0]
+        for i in range(1, 32):
+            v = v + ar_b[k, i]
+        ar_a[k, c * 8 + z] = v
+        for j in range(1, 16):
+            late_b_copy(k, j).start()
+
+    def late_end(k):
+        wait_bytes(ar_a.at[k, pl.ds(0, 15)], r_ara.at[k])
+        halves = []
+        for half in range(2):
+            v = ar_a[k, half * 8]
+            for i in range(1, 8):
+                v = v + ar_a[k, half * 8 + i]
+            halves.append(v)
+        return jnp.concatenate(halves, axis=1)
+
     def sum_sent(k):
         wait_bytes(ar_a.at[k, pl.ds(0, 15)], s_ara.at[k])
         wait_bytes(ar_b.at[k, pl.ds(0, 31)], s_arb.at[k])
 
-    core_copy = remote(pt.at[1 - c], core_in, s_core, r_core, partner)
+    def core_piece(n):
+        run = pl.ds(18 * n, 18 - 6 * n)
+        return remote(pt.at[1 - c, run], core_in.at[run], s_core.at[n], r_core.at[n], partner)
 
     def copy_ra(h, j):
         run = run4(h, j)
@@ -400,12 +484,13 @@
         )
 
     def core_sum():
-        core_copy.wait_recv()
-
-        @pl.loop(0, 32)
-        def _(s):
-            summed[s] = (pt[c, s].astype(F32) + core_in[s].astype(F32)).astype(BF16)
-
+        for s in (SPOT_OF[30], SPOT_OF[31]):
+            summed[s] = jnp.zeros((128, 128), BF16)
+        for n in range(2):
+            core_piece(n).wait_recv()
+            for o in range(18 * n, 18 + 12 * n):
+                v = pt[c, o].astype(F32) + core_in[o].astype(F32)
+                summed[SPOT_OF[o]] = v.astype(BF16)
         for j in range(1, 4):
             copy_ra(0, j).start()
             copy_ra(1, j).start()
@@ -461,20 +546,17 @@
             parts.append(jnp.sum(e_blk, axis=0, keepdims=True))
 
     def products(kind, src):
-        for n in range(5):
-            cols = slice(256 * n, 256 * n + 256)
-            p_blk = dot(w_unit[...], src[:, cols].astype(BF16)).astype(BF16)
-            for s in range(30):
-                o = square_at(s)
-                kp, f = o // 3, o % 3
-                if kp // 2 == n:
-                    lo = 128 * (kp % 2)
-                    pt[kind, s] = p_blk[128 * f:128 * f + 128, lo:lo + 128]
-
-    def empty_squares():
-        for kind in range(2):
-            for s in (30, 31):
-                pt[kind, s] = jnp.zeros((128, 128), BF16)
+        for n in range(2):
+            for half in range(3 * n, 3 + 2 * n):
+                cols = slice(256 * half, 256 * half + 256)
+                p_blk = dot(w_unit[...], src[:, cols].astype(BF16)).astype(BF16)
+                for k in range(6):
+                    lo, f = 128 * (k // 3), k % 3
+                    pt[kind, 6 * half + k] = p_blk[128 * f:128 * f + 128, lo:lo + 128]
+
+            @pl.when(c != kind)
+            def _():
+                core_piece(n).start()
 
     sum_start(0, tot)
 
@@ -496,11 +578,6 @@
     student(range(5))
     sum_start(3, jnp.concatenate(parts, axis=1))
     products(0, ex)
-    empty_squares()
-
-    @pl.when(c == 1)
-    def _():
-        core_copy.start()
 
     row = 1.0 / sum_end(0)
 
@@ -511,14 +588,15 @@
         return acc + fold8(k_blk * col)
 
     tot = fold1(lax.fori_loop(0, COLS // BLK, sweep, zero8))
-    sum_start(1, tot)
+    late_start(1, tot)
+    late_turn(1)
+    sum_turn(3)
 
     @pl.when(c == 0)
     def _():
         core_sum()
 
-    sum_turn(1)
-    row = 1.0 / sum_end(1)
+    row = 1.0 / late_end(1)
 
     def last_sweep(i, acc):
         rows = pl.ds(pl.multiple_of(i * BLK, BLK), BLK)
@@ -530,20 +608,18 @@
 
     acc_k, acc_l = lax.fori_loop(0, COLS // BLK, last_sweep, (zero8, zero8))
 
-    sum_start(2, fold1(acc_k))
-    sum_turn(3)
+    late_start(2, fold1(acc_k))
     products(1, kt)
 
     @pl.when(c == 0)
     def _():
-        core_copy.start()
         line_sums()
 
     @pl.when(c == 1)
     def _():
         core_sum()
 
-    sum_turn(2)
+    late_turn(2)
     partition = sum_end(3)
 
     @pl.when(c == 0)
@@ -554,7 +630,7 @@
     def _():
         line_sums()
 
-    row = 1.0 / sum_end(2)
+    row = 1.0 / late_end(2)
     row_w = jnp.concatenate([jnp.full((1, 128), w, F32) for w in ROW_W], axis=1)
     log_term = jnp.sum(row_w * jnp.log(partition), axis=1, keepdims=True)
     cross = jnp.sum(row_w * row * fold1(acc_l), axis=1, keepdims=True)
@@ -623,35 +699,21 @@
 
     @pl.when(sends_back)
     def _():
-        v = (whole[0] + whole[1]).T
+        v = whole[0] + whole[1]
         hi = v.astype(BF16)
         lo = (v - hi.astype(F32)).astype(BF16)
-        tiles[...] = (dot(sel[c], hi) + dot(sel[c], lo)).reshape(32, 16, 128)
-
-        @pl.loop(0, 32)
-        def _(i):
-            @pl.when(jnp.logical_not(stays(i)))
-            def _():
-                copy_back(i).start()
-
-            @pl.when(stays(i))
-            def _():
-                pltpu.make_async_copy(tiles.at[i], back.at[k_me, f_me], r_back).start()
-
-    for b in range(4):
-        @pl.when(y == b)
-        def _():
-            got = back.at[pl.ds(0, 4 - b)]
-            pltpu.make_async_copy(got, got, r_back).wait()
-            for k in range(4 - b, 4):
-                back[k] = jnp.zeros((3, 16, 128), F32)
-
-    cols = []
-    for f in range(3):
-        cols.append(back[0, f] + back[1, f] + back[2, f] + back[3, f])
-    gx = jnp.concatenate(cols, axis=1)
-    u = unit_f[y]
-    gr_ref[...] = (gx - u * jnp.sum(u * gx, axis=1, keepdims=True)) / norm_f[y][:, :1]
+        for q in range(4):
+            part_sel = sel[c, 128 * q:128 * q + 128]
+            t = dot_nt(part_sel, hi) + dot_nt(part_sel, lo)
+            tiles[8 * q:8 * q + 8] = t.reshape(8, 16, 128)
+            for i in range(8 * q, 8 * q + 8):
+                @pl.when(jnp.logical_not(stays(i)))
+                def _():
+                    copy_back(i).start()
+
+                @pl.when(stays(i))
+                def _():
+                    pltpu.make_async_copy(tiles.at[i], back.at[k_me, f_me], r_back).start()
 
     wait_bytes(ls_b.at[pl.ds(0, 15)], r_lsb)
     v = ls_b[0]
@@ -661,13 +723,17 @@
     store_loss = pltpu.make_async_copy(loss_ref, loss_hbm, s_loss)
     store_loss.start()
 
-    each_owner(raw_done, None)
+    each_owner(cnt_done, None)
+    each_owner(tile_done, None, (0,))
 
     @pl.when(is_owner)
     def _():
         pair_copy.wait_send()
-        for j in range(1, 8):
-            z_copy(j).wait_send()
+
+        @pl.when(c == 0)
+        def _():
+            for j in range(1, 8):
+                z_copy(j).wait_send()
 
     for h in range(2):
         for j in range(1, 4):
@@ -686,8 +752,24 @@
         sum_sent(k)
     wait_bytes(ls_a.at[pl.ds(0, 15)], s_lsa)
     wait_bytes(ls_b.at[pl.ds(0, 15)], s_lsb)
+    for n in range(2):
+        core_piece(n).wait_send()
+
+    for b in range(4):
+        @pl.when(y == b)
+        def _():
+            got = back.at[pl.ds(0, 4 - b)]
+            pltpu.make_async_copy(got, got, r_back).wait()
+            for k in range(4 - b, 4):
+                back[k] = jnp.zeros((3, 16, 128), F32)
+
+    cols = []
+    for f in range(3):
+        cols.append(back[0, f] + back[1, f] + back[2, f] + back[3, f])
+    gx = jnp.concatenate(cols, axis=1)
+    u = unit_f[y]
+    gr_ref[...] = (gx - u * jnp.sum(u * gx, axis=1, keepdims=True)) / norm_f[y][:, :1]
     store_loss.wait()
-    core_copy.wait_send()
 
     @pl.when(sends_back)
     def _():
@@ -734,8 +816,8 @@
         pltpu.VMEM((4, 32, 1, 640), F32),
         pltpu.VMEM((16, 1, 128), F32),
         pltpu.VMEM((16, 1, 128), F32),
-        pltpu.VMEM((2, 32, 128, 128), BF16),
-        pltpu.VMEM((32, 128, 128), BF16),
+        pltpu.VMEM((2, 30, 128, 128), BF16),
+        pltpu.VMEM((30, 128, 128), BF16),
         pltpu.VMEM((32, 128, 128), BF16),
         pltpu.VMEM((3, 4, 128, 128), BF16),
         pltpu.VMEM((3, 4, 128, 128), BF16),
@@ -753,11 +835,12 @@
         dma((7,)), dma((2,)),
         dma((2, 3)), dma((2, 3)), dma((2, 3)), dma((2, 3)), dma((2, 4)), dma((2, 4)),
         dma((4,)), dma((4,)), dma((4,)), dma((4,)), dma, dma, dma, dma,
-        dma, dma,
+        dma((2,)), dma((2,)),
         dma((2, 3)), dma((2, 3)), dma((2, 3)), dma((2, 3)), dma((2,)), dma((7,)),
         dma, dma,
         dma((32,)), dma,
         dma((5,)), dma,
+        pltpu.SemaphoreType.REGULAR,
     ]
     loss, grad_weight, grad_rows = pl.pallas_call(
         kernel,

time: 91.3 us -> 84.9 us (0.930); the launches traced: 89.6 us -> 84.8 us
  Pallas kernels: 85.8 us -> 81 us
    pallas_call x1, Pallas kernels: 85.8 us -> 81 us  [shards(): pl.pallas_call(kernel, out_shape=(jax.ShapeDtypeStruct((1, 1), F32), jax....]
where the time goes in v3:
time: 84.9 us; the launch traced here: 84.8 us
  Pallas kernels  81 us (95%)
  between operations  2.33 us (3%)
  local copies, waits for them, and re-layouts  1.49 us (2%)
    pallas_call x1, Pallas kernels, shards(): pl.pallas_call(kernel, out_shape=(jax.ShapeDtypeStruct((1, 1), F32), jax....  81 us

profile of v3, /device:TPU:6, one launch (start us, length us, event | category | flops | bytes accessed | tf_op | source)
XLA Modules:
  0.0 84.8 jit_solution(18090537163728436691)
XLA Ops:
  0.6 81.0 %shard_map.76 = (f32[1,1]{1,0:T(1,128)}, f32[384,512]{1,0:T(8,128)S(1)}, f32[16,384]{1,0:T(8,128)S(1)}) custom-call(bf16[1,128,384]{2,1,0:T(8,128)(2,1)} %sf_hbm.1, bf16[1,128,384]{2,1,0:T(8,128)(2,1)} %tf_hbm.1, bf16[384,512]{1,0:T(8,128)(2,1)} %sw_hbm.1, bf16[384,512]{1,0:T(8,128)(2,1)} %tw_hbm.1, s32[1,128]{1,0:T(1,128)} %mask_hbm.1), custom_call_target="tpu_custom_call" | custom-call | tf_op jit(solution)/shard_map/pallas_call | solution.py:845
  82.2 0.9 %copy.12 = f32[384,512]{1,0:T(8,128)} copy(f32[384,512]{1,0:T(8,128)S(1)} %get-tuple-element.13) | data formatting | bytes 1572864
  83.1 0.6 copy.13

commit v4 on v3

--- a/solution.py
+++ b/solution.py
@@ -59,7 +59,7 @@
     units, unit_f, norm_f, cnt, raw, rawc, sel, grid, tea, stu,
     w_unit, w_t, tw_t, w_norm, kt, lg, ex, gb, csum,
     ar_v, ar_a, ar_b, ls_a, ls_b,
-    pt, core_in, summed, in_a0, in_a1, half0, half1, in_b0, in_b1, quart, in_z,
+    pt, core_in, summed, in_a0, in_a1, half0, half1, in_b0, in_b1, quart_p, quart_t, in_zp, in_zt,
     scale, whole, tiles, back,
     s_raw, s_cnt, r_raw, r_cnt, s_z, r_z, s_2, r_2, s_3, r_3, s_ex, r_ex,
     s_ara, r_ara, s_arb, r_arb, s_lsa, r_lsa, s_lsb, r_lsb, s_core, r_core, s_ra, r_ra, s_rb, r_rb, s_rz, r_rz, s_pair, r_pair, s_back, r_back, s_in, s_loss, turn,
@@ -476,11 +476,14 @@
         spot = lax.rem((x if h == 0 else y) + j, 4)
         return remote(src.at[spot], dst.at[j - 1], s_rb.at[h, j - 1], r_rb.at[h, j - 1], dev)
 
-    def copy_rz(h):
+    quarts, in_zs = (quart_p, quart_t), (in_zp, in_zt)
+
+    def copy_rz(kind, h):
         away = lax.rem(x + 4 * h - z + 8, 8)
         slot = jnp.maximum(away - 1, 0)
         return remote(
-            quart.at[h], in_z.at[slot], s_rz.at[h], r_rz.at[slot], at(x, y, x + 4 * h, c)
+            quarts[kind].at[h], in_zs[kind].at[slot], s_rz.at[h], r_rz.at[slot],
+            at(x, y, x + 4 * h, c),
         )
 
     def core_sum():
@@ -508,7 +511,7 @@
             for j in range(1, 4):
                 copy_rb(h, j).start()
 
-    def plane_sums():
+    def plane_sums(kind):
         for h in range(2):
             for j in range(1, 4):
                 copy_rb(h, j).wait_recv()
@@ -517,20 +520,21 @@
             v = (half0, half1)[h][own].astype(F32)
             for j in range(3):
                 v = v + got[j].astype(F32)
-            quart[h] = v
+            quarts[kind][h] = v.astype(quarts[kind].dtype)
 
             @pl.when(z != x + 4 * h)
             def _():
-                copy_rz(h).start()
+                copy_rz(kind, h).start()
 
     pair_copy = remote(whole.at[c], whole.at[c], s_pair, r_pair, partner)
 
-    def finish_square():
+    def finish_square(kind):
+        src, got = quarts[kind], in_zs[kind]
         for j in range(1, 8):
-            remote(quart.at[0], in_z.at[j - 1], s_rz.at[0], r_rz.at[j - 1], partner).wait_recv()
-        v = quart[h_me]
+            remote(src.at[0], got.at[j - 1], s_rz.at[0], r_rz.at[j - 1], partner).wait_recv()
+        v = src[h_me].astype(F32)
         for j in range(7):
-            v = v + in_z[j]
+            v = v + got[j].astype(F32)
         whole[c] = v * scale[c, kp_me]
         pair_copy.start()
 
@@ -577,7 +581,6 @@
     assemble(0, stu)
     student(range(5))
     sum_start(3, jnp.concatenate(parts, axis=1))
-    products(0, ex)
 
     row = 1.0 / sum_end(0)
 
@@ -589,6 +592,7 @@
 
     tot = fold1(lax.fori_loop(0, COLS // BLK, sweep, zero8))
     late_start(1, tot)
+    products(0, ex)
     late_turn(1)
     sum_turn(3)
 
@@ -608,8 +612,8 @@
 
     acc_k, acc_l = lax.fori_loop(0, COLS // BLK, last_sweep, (zero8, zero8))
 
+    products(1, kt)
     late_start(2, fold1(acc_k))
-    products(1, kt)
 
     @pl.when(c == 0)
     def _():
@@ -622,15 +626,16 @@
     late_turn(2)
     partition = sum_end(3)
 
+    @pl.when(c == 1)
+    def _():
+        line_sums()
+
+    row = 1.0 / late_end(2)
+
     @pl.when(c == 0)
     def _():
-        plane_sums()
-
-    @pl.when(c == 1)
-    def _():
-        line_sums()
-
-    row = 1.0 / late_end(2)
+        plane_sums(0)
+
     row_w = jnp.concatenate([jnp.full((1, 128), w, F32) for w in ROW_W], axis=1)
     log_term = jnp.sum(row_w * jnp.log(partition), axis=1, keepdims=True)
     cross = jnp.sum(row_w * row * fold1(acc_l), axis=1, keepdims=True)
@@ -653,10 +658,6 @@
     scale[0, 10] = jnp.zeros((1, 128), F32)
     scale[1, 10] = jnp.zeros((1, 128), F32)
 
-    @pl.when(is_owner & (c == 0))
-    def _():
-        finish_square()
-
     @pl.loop(0, COLS // BLK)
     def _(i):
         rows = pl.ds(pl.multiple_of(i * BLK, BLK), BLK)
@@ -664,7 +665,7 @@
 
     @pl.when(c == 1)
     def _():
-        plane_sums()
+        plane_sums(1)
 
     gu = dot(gb[...], stu[...]).T
     w_f = w_unit[...].astype(F32)
@@ -683,15 +684,19 @@
 
     def copy_back(i):
         return remote(
-            tiles.at[i], back.at[k_me, f_me], s_back.at[i], r_back, (2 * i + c, b_me)
+            tiles.at[i], back.at[k_me, f_me], s_back, r_back, (2 * i + c, b_me)
         )
 
     def stays(i):
         return (2 * i + c == img) & (b_me == y)
 
+    @pl.when(is_owner & (c == 0))
+    def _():
+        finish_square(0)
+
     @pl.when(is_owner & (c == 1))
     def _():
-        finish_square()
+        finish_square(1)
 
     @pl.when(is_owner)
     def _():
@@ -744,9 +749,10 @@
         for j in range(4):
             copy_ex(h, j, c).wait_send()
 
-        @pl.when(z != x + 4 * h)
-        def _():
-            copy_rz(h).wait_send()
+        for kind in range(2):
+            @pl.when((z != x + 4 * h) & (c == kind))
+            def _():
+                copy_rz(kind, h).wait_send()
 
     for k in range(4):
         sum_sent(k)
@@ -754,6 +760,14 @@
     wait_bytes(ls_b.at[pl.ds(0, 15)], s_lsb)
     for n in range(2):
         core_piece(n).wait_send()
+
+    @pl.when(sends_back & (b_me == y))
+    def _():
+        wait_bytes(tiles.at[pl.ds(0, 31)], s_back)
+
+    @pl.when(sends_back & (b_me != y))
+    def _():
+        wait_bytes(tiles, s_back)
 
     for b in range(4):
         @pl.when(y == b)
@@ -770,14 +784,6 @@
     u = unit_f[y]
     gr_ref[...] = (gx - u * jnp.sum(u * gx, axis=1, keepdims=True)) / norm_f[y][:, :1]
     store_loss.wait()
-
-    @pl.when(sends_back)
-    def _():
-        @pl.loop(0, 32)
-        def _(i):
-            @pl.when(jnp.logical_not(stays(i)))
-            def _():
-                copy_back(i).wait_send()
 
 
 def shards(student_feats, teacher_feats, student_weight, teacher_weight, patch_masks):
@@ -826,7 +832,9 @@
         pltpu.VMEM((3, 128, 128), BF16),
         pltpu.VMEM((3, 128, 128), BF16),
         pltpu.VMEM((2, 128, 128), F32),
+        pltpu.VMEM((2, 128, 128), BF16),
         pltpu.VMEM((7, 128, 128), F32),
+        pltpu.VMEM((7, 128, 128), BF16),
         pltpu.VMEM((2, 11, 1, 128), F32),
         pltpu.VMEM((2, 128, 128), F32),
         pltpu.VMEM((32, 16, 128), F32),
@@ -838,7 +846,7 @@
         dma((2,)), dma((2,)),
         dma((2, 3)), dma((2, 3)), dma((2, 3)), dma((2, 3)), dma((2,)), dma((7,)),
         dma, dma,
-        dma((32,)), dma,
+        dma, dma,
         dma((5,)), dma,
         pltpu.SemaphoreType.REGULAR,
     ]

time: 84.9 us -> 85.3 us (level)
  no operation moved by 1% of the time
where the time goes in v4:
time: 85.3 us; the launch traced here: 85.2 us
  Pallas kernels  81.4 us (95%)
  between operations  2.33 us (3%)
  local copies, waits for them, and re-layouts  1.49 us (2%)
    pallas_call x1, Pallas kernels, shards(): pl.pallas_call(kernel, out_shape=(jax.ShapeDtypeStruct((1, 1), F32), jax....  81.4 us

profile of v4, /device:TPU:6, one launch (start us, length us, event | category | flops | bytes accessed | tf_op | source)
XLA Modules:
  0.0 85.2 jit_solution(10019972723353399272)
XLA Ops:
  0.6 81.4 %shard_map.76 = (f32[1,1]{1,0:T(1,128)}, f32[384,512]{1,0:T(8,128)S(1)}, f32[16,384]{1,0:T(8,128)S(1)}) custom-call(bf16[1,128,384]{2,1,0:T(8,128)(2,1)} %sf_hbm.1, bf16[1,128,384]{2,1,0:T(8,128)(2,1)} %tf_hbm.1, bf16[384,512]{1,0:T(8,128)(2,1)} %sw_hbm.1, bf16[384,512]{1,0:T(8,128)(2,1)} %tw_hbm.1, s32[1,128]{1,0:T(1,128)} %mask_hbm.1), custom_call_target="tpu_custom_call" | custom-call | tf_op jit(solution)/shard_map/pallas_call | solution.py:853
  82.6 0.9 %copy.12 = f32[384,512]{1,0:T(8,128)} copy(f32[384,512]{1,0:T(8,128)S(1)} %get-tuple-element.13) | data formatting | bytes 1572864
  83.4 0.6 copy.13

commit v5 on v4

--- a/solution.py
+++ b/solution.py
@@ -626,20 +626,20 @@
     late_turn(2)
     partition = sum_end(3)
 
+    @pl.when(c == 0)
+    def _():
+        plane_sums(0)
+
+
     @pl.when(c == 1)
     def _():
         line_sums()
 
     row = 1.0 / late_end(2)
-
-    @pl.when(c == 0)
-    def _():
-        plane_sums(0)
-
     row_w = jnp.concatenate([jnp.full((1, 128), w, F32) for w in ROW_W], axis=1)
     log_term = jnp.sum(row_w * jnp.log(partition), axis=1, keepdims=True)
     cross = jnp.sum(row_w * row * fold1(acc_l), axis=1, keepdims=True)
-    ls_a[zc] = jnp.broadcast_to(cross, (1, 128))
+    ls_b[xy] = jnp.broadcast_to(cross, (1, 128))
 
     def ls_a_copy(j):
         return remote(ls_a.at[zc], ls_a.at[zc], s_lsa, r_lsa, zc_peer(j)[0])
@@ -648,7 +648,7 @@
         return remote(ls_b.at[xy], ls_b.at[xy], s_lsb, r_lsb, xy_peer(j))
 
     for j in range(1, 16):
-        ls_a_copy(j).start()
+        ls_b_copy(j).start()
     lead = row_w * (ROWS / STUDENT_TEMP)
     scale_p = lead / partition
     scale_t = lead * row
@@ -672,13 +672,13 @@
     gw_ref[...] = (
         1024.0 * (gu - w_f * jnp.sum(w_f * gu, axis=0, keepdims=True)) / w_norm[...]
     )
-    wait_bytes(ls_a.at[pl.ds(0, 15)], r_lsa)
-    v = ls_a[0]
+    wait_bytes(ls_b.at[pl.ds(0, 15)], r_lsb)
+    v = ls_b[0]
     for i in range(1, 16):
-        v = v + ls_a[i]
-    ls_b[xy] = v
+        v = v + ls_b[i]
+    ls_a[zc] = v
     for j in range(1, 16):
-        ls_b_copy(j).start()
+        ls_a_copy(j).start()
 
     sends_back = is_owner & (o_me < 30)
 
@@ -720,10 +720,10 @@
                 def _():
                     pltpu.make_async_copy(tiles.at[i], back.at[k_me, f_me], r_back).start()
 
-    wait_bytes(ls_b.at[pl.ds(0, 15)], r_lsb)
-    v = ls_b[0]
+    wait_bytes(ls_a.at[pl.ds(0, 15)], r_lsa)
+    v = ls_a[0]
     for i in range(1, 16):
-        v = v + ls_b[i]
+        v = v + ls_a[i]
     loss_ref[...] = log_term - v[:, :1]
     store_loss = pltpu.make_async_copy(loss_ref, loss_hbm, s_loss)
     store_loss.start()

time: 85.3 us -> 83.5 us (0.979)
  Pallas kernels: 81.4 us -> 79.5 us
    pallas_call x1, Pallas kernels: 81.4 us -> 79.5 us  [shards(): pl.pallas_call(kernel, out_shape=(jax.ShapeDtypeStruct((1, 1), F32), jax....]
where the time goes in v5:
time: 83.5 us; the launch traced here: 83.3 us
  Pallas kernels  79.5 us (95%)
  between operations  2.33 us (3%)
  local copies, waits for them, and re-layouts  1.49 us (2%)
    pallas_call x1, Pallas kernels, shards(): pl.pallas_call(kernel, out_shape=(jax.ShapeDtypeStruct((1, 1), F32), jax....  79.5 us

profile of v5, /device:TPU:6, one launch (start us, length us, event | category | flops | bytes accessed | tf_op | source)
XLA Modules:
  0.0 83.3 jit_solution(13377392661121623865)
XLA Ops:
  0.6 79.5 %shard_map.76 = (f32[1,1]{1,0:T(1,128)}, f32[384,512]{1,0:T(8,128)S(1)}, f32[16,384]{1,0:T(8,128)S(1)}) custom-call(bf16[1,128,384]{2,1,0:T(8,128)(2,1)} %sf_hbm.1, bf16[1,128,384]{2,1,0:T(8,128)(2,1)} %tf_hbm.1, bf16[384,512]{1,0:T(8,128)(2,1)} %sw_hbm.1, bf16[384,512]{1,0:T(8,128)(2,1)} %tw_hbm.1, s32[1,128]{1,0:T(1,128)} %mask_hbm.1), custom_call_target="tpu_custom_call" | custom-call | tf_op jit(solution)/shard_map/pallas_call | solution.py:853
  80.7 0.9 %copy.12 = f32[384,512]{1,0:T(8,128)} copy(f32[384,512]{1,0:T(8,128)S(1)} %get-tuple-element.13) | data formatting | bytes 1572864
  81.6 0.6 copy.13

commit v6 on v5

--- a/solution.py
+++ b/solution.py
@@ -11,7 +11,7 @@
 STUDENT_TEMP = 0.1
 NORM_EPS = 1e-06
 ROWS, COLS, E, ITERS = 1280, 512, 384, 3
-BLK = 128
+BLK = 256
 GROUPS = [(b, m) for b in range(4) for m in range(b + 1, 5)]
 ROW_W = [1.0 / (16.0 * m * 32.0) for _, m in GROUPS]
 

time: 83.5 us -> 82.9 us (level)
  no operation moved by 1% of the time
where the time goes in v6:
time: 82.9 us; the launch traced here: 82.7 us
  Pallas kernels  78.9 us (95%)
  between operations  2.33 us (3%)
  local copies, waits for them, and re-layouts  1.49 us (2%)
    pallas_call x1, Pallas kernels, shards(): pl.pallas_call(kernel, out_shape=(jax.ShapeDtypeStruct((1, 1), F32), jax....  78.9 us

profile of v6, /device:TPU:6, one launch (start us, length us, event | category | flops | bytes accessed | tf_op | source)
XLA Modules:
  0.0 82.7 jit_solution(2274367865748471616)
XLA Ops:
  0.6 78.9 %shard_map.76 = (f32[1,1]{1,0:T(1,128)}, f32[384,512]{1,0:T(8,128)S(1)}, f32[16,384]{1,0:T(8,128)S(1)}) custom-call(bf16[1,128,384]{2,1,0:T(8,128)(2,1)} %sf_hbm.1, bf16[1,128,384]{2,1,0:T(8,128)(2,1)} %tf_hbm.1, bf16[384,512]{1,0:T(8,128)(2,1)} %sw_hbm.1, bf16[384,512]{1,0:T(8,128)(2,1)} %tw_hbm.1, s32[1,128]{1,0:T(1,128)} %mask_hbm.1), custom_call_target="tpu_custom_call" | custom-call | tf_op jit(solution)/shard_map/pallas_call | solution.py:853
  80.1 0.9 %copy.12 = f32[384,512]{1,0:T(8,128)} copy(f32[384,512]{1,0:T(8,128)S(1)} %get-tuple-element.13) | data formatting | bytes 1572864
  81.0 0.6 copy.13
